TPU v7x, 32 devices: a whole 2x2x4 slice. The times are simulated.
32 devices in a mesh: dp: 8 (over z, y), shard: 4 (over x, core).
Axes of the slice: x: 2, y: 2, z: 4, core: 2. Of those that a mesh axis runs over, the one named last changes fastest.
Arguments:
- embedded: bfloat16 [30720, 1280], P(('dp', 'shard')), may hold values from -6 to 6
- mask_token_embedding: bfloat16 [1280], replicated, may hold values from -5 to 5
- destination: int32 [30720], P(('dp', 'shard')), may hold values from 0 to 8, as said below
- position: int32 [30720], P(('dp', 'shard')), may hold values from 0 to 79, as said below
- length: int32 [30720], P(('dp', 'shard')), may hold values from 0 to 80, as said below
- unmask_order: int32 [30720], P(('dp', 'shard')), may hold values from 0 to 79, as said below
- timestep: int32 [30720], P(('dp', 'shard')), may hold values from 0 to 80, as said below
- upstream: bfloat16 [12288, 1280], P(('dp', 'shard')), may hold values from -0.29882812 to 0.29882812
- gain_in: float32 [1280], replicated, may hold values from 0.4 to 1.6
- weight_in: bfloat16 [1280, 640], replicated, may hold values from -0.15625 to 0.15625
- gain_mid: float32 [640], replicated, may hold values from 0.4 to 1.6
- weight_conv: bfloat16 [640, 5, 640], replicated, may hold values from -0.109375 to 0.109375
- gain_out: float32 [640], replicated, may hold values from 0.4 to 1.6
- weight_out: bfloat16 [1280, 640], replicated, may hold values from -0.25 to 0.25
Outputs:
- grad_input: bfloat16 [12288, 1280], P(('dp', 'shard'))
- grad_weight_in: float32 [1280, 640], P('dp', 'shard')
- grad_weight_conv: float32 [640, 5, 640], P('dp', None, 'shard')
- grad_weight_out: float32 [1280, 640], P('dp', 'shard')
Inputs may be any that keep to these rules, and one draw needn't show every extreme that they name: 8 marks an empty slot. All slots of a sequence share one destination. Among the devices of one shard index, every destination receives exactly 384 rows, and one device sends one destination at most one sequence. A device's slots hold whole sequences one after another from its first slot, each in order of position; empty slots come last and hold 0. `length`: 0 on empty slots; equal on all slots of a sequence; every destination receives one sequence of exactly 80 residues. `unmask_order`: within each sequence a permutation of its positions; 0 on empty slots. `timestep`: equal on all slots of a sequence, from 1 to its length; 0 on empty slots.
All inputs are finite; a program needn't handle non-finite values.
Results may differ from a plain program's by a relative error of at most 0.0074.
Values may be sent and summed in bfloat16 or wider, within the bound.
A program may use at most 192 MiB of HBM per device.

v0:
```python
import jax
import jax.numpy as jnp
from jax import lax
from jax.experimental import pallas as pl
from jax.experimental.pallas import tpu as pltpu
import functools
from jax.sharding import PartitionSpec as P

KERNEL_TAPS = 5
DILATION_STEP = 16
LMAX = 80


EPS = 1e-05


def normalized_activation(values, gain_vec):
    row_mean = jnp.mean(values, axis=-1, keepdims=True)
    centred = values - row_mean
    row_var = jnp.mean(centred * centred, axis=-1, keepdims=True)
    return jax.nn.gelu(centred * lax.rsqrt(row_var + EPS) * gain_vec, approximate=False)


def raw_shift(values, offset):
    if offset > 0:
        filler = jnp.zeros((offset, values.shape[1]), values.dtype)
        return jnp.concatenate([values[offset:], filler], axis=0)
    if offset < 0:
        filler = jnp.zeros((-offset, values.shape[1]), values.dtype)
        return jnp.concatenate([filler, values[:offset]], axis=0)
    return values


def contract_rows(left, right):
    return lax.dot_general(
        left, right, (((0,), (0,)), ((), ())), preferred_element_type=jnp.float32
    )


def contract_cols(left, right):
    return lax.dot_general(
        left, right, (((1,), (1,)), ((), ())), preferred_element_type=jnp.float32
    )


def layer_grads(
    owner_input,
    upstream,
    owner_position,
    owner_length,
    gain_in,
    weight_in,
    gain_mid,
    weight_conv,
    gain_out,
    weight_out,
):
    widened_input = owner_input.astype(jnp.float32)
    first_f32 = normalized_activation(widened_input, gain_in)
    first_act = first_f32.astype(jnp.bfloat16)
    hidden = jnp.dot(first_act, weight_in, preferred_element_type=jnp.float32)
    mid_f32, pull_mid = jax.vjp(lambda value: normalized_activation(value, gain_mid), hidden)
    mid_act = mid_f32.astype(jnp.bfloat16)
    tap_offsets = [
        (kernel_tap_index - KERNEL_TAPS // 2) * DILATION_STEP
        for kernel_tap_index in range(KERNEL_TAPS)
    ]
    tap_valid = [
        (owner_position + offset >= 0) & (owner_position + offset < owner_length)
        for offset in tap_offsets
    ]
    tap_list = [
        jnp.where(
            tap_valid[kernel_tap_index][:, None],
            raw_shift(mid_act, tap_offsets[kernel_tap_index]),
            jnp.zeros_like(mid_act),
        )
        for kernel_tap_index in range(KERNEL_TAPS)
    ]
    conv = jnp.dot(tap_list[0], weight_conv[:, 0, :], preferred_element_type=jnp.float32)
    for kernel_tap_index in range(1, KERNEL_TAPS):
        conv = conv + jnp.dot(
            tap_list[kernel_tap_index],
            weight_conv[:, kernel_tap_index, :],
            preferred_element_type=jnp.float32,
        )
    out_f32, pull_out = jax.vjp(lambda value: normalized_activation(value, gain_out), conv)
    out_act = out_f32.astype(jnp.bfloat16)
    out_cot = jnp.dot(upstream, weight_out, preferred_element_type=jnp.float32)
    conv_cot = pull_out(out_cot)[0].astype(jnp.bfloat16)
    mid_cot = jnp.zeros(mid_act.shape, jnp.float32)
    for kernel_tap_index in range(KERNEL_TAPS):
        back_term = contract_cols(conv_cot, weight_conv[:, kernel_tap_index, :])
        back_term = jnp.where(
            tap_valid[kernel_tap_index][:, None], back_term, jnp.zeros_like(back_term)
        )
        mid_cot = mid_cot + raw_shift(back_term, -tap_offsets[kernel_tap_index])
    hidden_cot = pull_mid(mid_cot)[0].astype(jnp.bfloat16)
    return (first_act, mid_act, out_act, conv_cot, hidden_cot)


MESH = pl.DeviceIdType.MESH


def bit_orders(owners, groups):
    dp_bits = [("dp", i) for i in range(owners.bit_length() - 1)]
    sh_bits = [("shard", i) for i in range(groups.bit_length() - 1)]
    first, others = sh_bits[:1], sh_bits[1:]
    return (
        first + others + dp_bits,
        first + dp_bits[:1] + others + dp_bits[1:],
        first + dp_bits[1:] + others + dp_bits[:1],
    )


def chunk_rows(rows):
    unit = rows // 5
    return (2 * unit, 2 * unit, unit)


def round_up(value, multiple):
    return -(-value // multiple) * multiple


def placed(values, offset):
    low = offset // 128 * 128
    high = round_up(offset + values.shape[1], 128)
    parts = []
    if offset > low:
        parts.append(jnp.zeros((values.shape[0], offset - low), values.dtype))
    parts.append(values)
    if high > offset + values.shape[1]:
        parts.append(jnp.zeros((values.shape[0], high - offset - values.shape[1]), values.dtype))
    return low, (jnp.concatenate(parts, axis=1) if len(parts) > 1 else values)


FILL = 64.0
INV_SQRT2 = 0.7071067811865476
INV_SQRT_2PI = 0.3989422804014327
VMEM_LIMIT = 60 * 1024 * 1024


def flipped(index, mask):
    other, bit = index, 0
    while (mask >> bit) > 0:
        if (mask >> bit) & 1:
            other = other + (1 - 2 * lax.rem(index // (1 << bit), 2)) * (1 << bit)
        bit += 1
    return other


def dispatch_kernel(
    owners,
    destination,
    position,
    order,
    timestep,
    token,
    embedded,
    bucket,
    bucket_pos,
    bucket_len,
    sent,
    got,
    send_sem,
    recv_sem,
):
    me, group = lax.axis_index("dp"), lax.axis_index("shard")
    barrier = pltpu.get_barrier_semaphore()
    for j in range(1, owners):
        pl.semaphore_signal(
            barrier, inc=1, device_id=(flipped(me, j), group), device_id_type=MESH
        )
    slot = jnp.where(destination[...] < owners, destination[...] * LMAX + position[...], -1)
    hidden_slot = (order[...] < timestep[...]).astype(jnp.float32)

    def block_for(owner):
        rows = lax.broadcasted_iota(jnp.int32, (LMAX, slot.shape[1]), 0) + owner * LMAX
        pick = (rows == slot).astype(jnp.float32)
        live = jnp.sum(pick, axis=1, keepdims=True)
        masked = jnp.sum(pick * hidden_slot, axis=1, keepdims=True)
        block = jnp.dot(
            pick.astype(jnp.bfloat16), embedded[...], preferred_element_type=jnp.float32
        )
        block = jnp.where(masked > 0.5, token[...].astype(jnp.float32), block)
        return jnp.where(live > 0.5, block, FILL).astype(jnp.bfloat16)

    copies = []
    for j in range(owners - 1, 0, -1):
        other = flipped(me, j)
        sent[j] = block_for(other)
        if j == owners - 1:
            pl.semaphore_wait(barrier, owners - 1)
        copy = pltpu.make_async_remote_copy(
            src_ref=sent.at[j],
            dst_ref=got.at[me],
            send_sem=send_sem.at[j],
            recv_sem=recv_sem.at[j],
            device_id=(other, group),
            device_id_type=MESH,
        )
        copy.start()
        copies.append(copy)
    got[me] = block_for(me)
    for copy in copies:
        copy.wait_recv()
    lanes = lax.broadcasted_iota(jnp.int32, (1, owners * LMAX), 1)
    place_of = jnp.full((1, owners * LMAX), -1, jnp.int32)
    pos_of = jnp.zeros((1, owners * LMAX), jnp.float32)
    len_of = jnp.zeros((1, owners * LMAX), jnp.float32)
    start = jnp.zeros((1, 1), jnp.int32)
    for source in range(owners):
        marks = got[source, :, 0:128].astype(jnp.float32)[:, 0:1]
        count = jnp.sum((marks < FILL / 2).astype(jnp.float32), axis=0, keepdims=True)
        whole = count.astype(jnp.int32)
        inside = lanes - source * LMAX
        used = (inside >= 0) & (inside < whole)
        place_of = jnp.where(used, start + inside, place_of)
        pos_of = jnp.where(used, inside.astype(jnp.float32), pos_of)
        len_of = jnp.where(used, count, len_of)
        start = start + whole
    own = bucket.shape[0]
    take = (
        lax.broadcasted_iota(jnp.int32, (own, owners * LMAX), 0) == place_of
    ).astype(jnp.float32)
    bucket_pos[...] = jnp.sum(take * pos_of, axis=1, keepdims=True).astype(jnp.int32)
    bucket_len[...] = jnp.sum(take * len_of, axis=1, keepdims=True).astype(jnp.int32)
    bucket[...] = jnp.dot(
        take.astype(jnp.bfloat16),
        got[...].reshape(owners * LMAX, bucket.shape[1]),
        preferred_element_type=jnp.float32,
    ).astype(jnp.bfloat16)
    for copy in copies:
        copy.wait_send()


def gradient_kernel(
    owners,
    groups,
    position,
    length,
    mid,
    conv_cot,
    first,
    hidden_cot,
    upstream,
    out_act,
    weight_in,
    owner_input,
    gain_in,
    grad_input,
    grad_in,
    grad_conv,
    grad_out,
    *scratch,
):
    chunks = 3
    terms, got, sums = scratch[:chunks], scratch[chunks : 2 * chunks], scratch[2 * chunks : 9]
    lefts, rights, input_cot, send_sem, recv_sem = (
        scratch[9:12],
        scratch[12:15],
        scratch[15],
        scratch[16],
        scratch[17],
    )
    orders = bit_orders(owners, groups)
    steps = len(orders[0])
    total = 1 << steps
    me = {"dp": lax.axis_index("dp"), "shard": lax.axis_index("shard")}

    def bit_of(axis, bit):
        return lax.rem(me[axis] // (1 << bit), 2)

    def partner(axis, bit):
        other = me[axis] + (1 - 2 * bit_of(axis, bit)) * (1 << bit)
        return (other, me["shard"]) if axis == "dp" else (me["dp"], other)

    barrier = pltpu.get_barrier_semaphore()
    for axis, bit in orders[0]:
        pl.semaphore_signal(barrier, inc=1, device_id=partner(axis, bit), device_id_type=MESH)

    narrow, wide = mid.shape[1] // owners, first.shape[1] // owners
    rows = conv_cot.shape[1] // groups
    width = terms[0].shape[2]
    offsets = (0, KERNEL_TAPS * narrow, KERNEL_TAPS * narrow + wide)
    taps = []
    for k in range(KERNEL_TAPS):
        offset = (k - KERNEL_TAPS // 2) * DILATION_STEP
        moved = position[...] + offset
        valid = (moved >= 0) & (moved < length[...])
        shifted = raw_shift(mid[...], offset).astype(jnp.float32)
        taps.append(jnp.where(valid, shifted, 0.0))
    for right, values in zip(rights, (conv_cot, hidden_cot, out_act)):
        right[...] = values[...].T
    for owner in range(owners):
        here = slice(owner * narrow, (owner + 1) * narrow)
        there = slice(owner * wide, (owner + 1) * wide)
        parts = (
            jnp.concatenate([t[:, here] for t in taps], axis=1),
            first[:, there].astype(jnp.float32),
            upstream[:, there].astype(jnp.float32),
        )
        for left, values, offset in zip(lefts, parts, offsets):
            left[owner] = placed(values, offset)[1].astype(jnp.bfloat16)

    def half_terms(low_bit):
        starts = [(2 * i + low_bit) * rows for i in range(groups // 2)]

        def body(owner, carry):
            tiles = [None] * (width // 128)
            for left, right, offset in zip(lefts, rights, offsets):
                low = offset // 128
                picked = [right[pl.ds(pl.multiple_of(s, 16), rows), :] for s in starts]
                picked = picked[0] if len(picked) == 1 else jnp.concatenate(picked, axis=0)
                term = jnp.dot(picked, left[owner], preferred_element_type=jnp.float32)
                for j in range(left.shape[2] // 128):
                    piece = term[:, j * 128 : (j + 1) * 128]
                    held = tiles[low + j]
                    tiles[low + j] = piece if held is None else held + piece
            for j, tile in enumerate(tiles):
                tile = tile.astype(jnp.bfloat16)
                for i in range(groups // 2):
                    at = i * rows
                    for order, out in zip(orders, terms):
                        index = low_bit
                        for axis, bit in order[1:]:
                            if axis == "dp":
                                index = index * 2 + lax.rem(owner // (1 << bit), 2)
                            else:
                                index = index * 2 + (((2 * i) >> bit) & 1)
                        count = out.shape[1]
                        out[index, :, j * 128 : (j + 1) * 128] = tile[at : at + count]
                        at += count
            return carry

        lax.fori_loop(0, owners, body, 0)

    base, at = [], 0
    for t in range(steps):
        base.append(at)
        at += total >> (t + 1)

    def copy_of(c, t):
        half = total >> (t + 1)
        away = 1 - bit_of(*orders[c][t])
        source = terms[c] if t == 0 else sums[c]
        start = away * half if t == 0 else base[t - 1] + away * half
        return pltpu.make_async_remote_copy(
            src_ref=source.at[pl.ds(start, half)],
            dst_ref=got[c].at[pl.ds(base[t], half)],
            send_sem=send_sem.at[c, t],
            recv_sem=recv_sem.at[c, t],
            device_id=partner(*orders[c][t]),
            device_id_type=MESH,
        )

    def summed(c, t, at):
        half = total >> (t + 1)
        kept = bit_of(*orders[c][t]) * half
        source = terms[c] if t == 0 else sums[c]
        offset = kept if t == 0 else base[t - 1] + kept
        return source[offset + at].astype(jnp.float32) + got[c][base[t] + at].astype(jnp.float32)

    def add(c, t, first_block, count):
        def body(i, carry):
            at = first_block + i
            sums[c][base[t] + at] = summed(c, t, at).astype(jnp.bfloat16)
            return carry

        lax.fori_loop(0, count, body, 0)

    def input_gradient():
        input_cot[...] = contract_cols(hidden_cot[...], weight_in[...])
        step_rows = 16

        def body(i, carry):
            at = pl.ds(pl.multiple_of(i * step_rows, step_rows), step_rows)
            value = owner_input[at, :].astype(jnp.float32)
            centred = value - jnp.mean(value, axis=-1, keepdims=True)
            scale = lax.rsqrt(jnp.mean(centred * centred, axis=-1, keepdims=True) + EPS)
            normal = centred * scale
            gain = gain_in[...]
            scaled = normal * gain
            slope = 0.5 * (1.0 + lax.erf(scaled * INV_SQRT2)) + scaled * (
                INV_SQRT_2PI * jnp.exp(-0.5 * scaled * scaled)
            )
            cot = input_cot[at, :] * slope * gain
            grad = scale * (
                cot
                - jnp.mean(cot, axis=-1, keepdims=True)
                - normal * jnp.mean(cot * normal, axis=-1, keepdims=True)
            )
            grad_input[at, :] = (upstream[at, :].astype(jnp.float32) + grad).astype(
                jnp.bfloat16
            )
            return carry

        lax.fori_loop(0, owner_input.shape[0] // step_rows, body, 0)

    mine = bit_of(*orders[0][0])
    half_terms(1 - mine)
    pl.semaphore_wait(barrier, steps)
    copies = [[copy_of(c, t) for t in range(steps)] for c in range(chunks)]
    for c in range(chunks):
        copies[c][0].start()
    half_terms(mine)
    for t in range(steps - 1):
        half = total >> (t + 2)
        for c in range(chunks):
            copies[c][t].wait_recv()
            nxt = bit_of(*orders[c][t + 1])
            add(c, t, (1 - nxt) * half, half)
            copies[c][t + 1].start()
            add(c, t, nxt * half, half)
        if t == 0:
            input_gradient()
    finished = []
    for c in range(chunks):
        copies[c][steps - 1].wait_recv()
        finished.append(summed(c, steps - 1, 0))
    result = jnp.concatenate(finished, axis=0).T
    for k in range(KERNEL_TAPS):
        grad_conv[:, k, :] = result[k * narrow : (k + 1) * narrow]
    grad_in[...] = result[offsets[1] : offsets[1] + wide]
    grad_out[...] = result[offsets[2] : offsets[2] + wide]
    for c in range(chunks):
        for t in range(steps):
            copies[c][t].wait_send()


def local(
    embedded,
    mask_token_embedding,
    destination,
    position,
    length,
    unmask_order,
    timestep,
    upstream,
    gain_in,
    weight_in,
    gain_mid,
    weight_conv,
    gain_out,
    weight_out,
):
    channels = embedded.shape[1]
    owners, groups = lax.axis_size("dp"), lax.axis_size("shard")
    own_rows = upstream.shape[0]
    inner = weight_in.shape[1]
    vmem = pl.BlockSpec(memory_space=pltpu.VMEM)
    bucket, bucket_pos, bucket_len = pl.pallas_call(
        functools.partial(dispatch_kernel, owners),
        out_shape=[
            jax.ShapeDtypeStruct((own_rows, channels), jnp.bfloat16),
            jax.ShapeDtypeStruct((own_rows, 1), jnp.int32),
            jax.ShapeDtypeStruct((own_rows, 1), jnp.int32),
        ],
        in_specs=[vmem] * 6,
        out_specs=[vmem] * 3,
        scratch_shapes=[
            pltpu.VMEM((owners, LMAX, channels), jnp.bfloat16),
            pltpu.VMEM((owners, LMAX, channels), jnp.bfloat16),
            pltpu.SemaphoreType.DMA((owners,)),
            pltpu.SemaphoreType.DMA((owners,)),
        ],
        compiler_params=pltpu.CompilerParams(
            collective_id=1, has_side_effects=True, vmem_limit_bytes=VMEM_LIMIT
        ),
        name="dispatch",
    )(
        destination[None, :],
        position[None, :],
        unmask_order[None, :],
        timestep[None, :],
        mask_token_embedding[None, :],
        embedded,
    )
    first_act, mid_act, out_act, conv_cot, hidden_cot = layer_grads(
        bucket,
        upstream,
        bucket_pos[:, 0],
        bucket_len[:, 0],
        gain_in,
        weight_in,
        gain_mid,
        weight_conv,
        gain_out,
        weight_out,
    )
    narrow, wide, rows = inner // owners, channels // owners, inner // groups
    offsets = (0, KERNEL_TAPS * narrow, KERNEL_TAPS * narrow + wide)
    sizes = (KERNEL_TAPS * narrow, wide, wide)
    spans = [round_up(o + n, 128) - o // 128 * 128 for o, n in zip(offsets, sizes)]
    width = round_up(offsets[2] + wide, 128)
    total = owners * groups
    steps = total.bit_length() - 1
    counts = chunk_rows(rows)
    outs = pl.pallas_call(
        functools.partial(gradient_kernel, owners, groups),
        out_shape=[
            jax.ShapeDtypeStruct((own_rows, channels), jnp.bfloat16),
            jax.ShapeDtypeStruct((wide, rows), jnp.float32),
            jax.ShapeDtypeStruct((narrow, KERNEL_TAPS, rows), jnp.float32),
            jax.ShapeDtypeStruct((wide, rows), jnp.float32),
        ],
        in_specs=[vmem] * 11,
        out_specs=[vmem] * 4,
        scratch_shapes=[pltpu.VMEM((total, n, width), jnp.bfloat16) for n in counts]
        + [pltpu.VMEM((total - 1, n, width), jnp.bfloat16) for n in counts]
        + [pltpu.VMEM((total - 1, n, width), jnp.bfloat16) for n in counts]
        + [pltpu.VMEM((owners, own_rows, n), jnp.bfloat16) for n in spans]
        + [pltpu.VMEM((inner, own_rows), jnp.bfloat16)] * 3
        + [pltpu.VMEM((own_rows, channels), jnp.float32)]
        + [pltpu.SemaphoreType.DMA((3, steps)), pltpu.SemaphoreType.DMA((3, steps))],
        compiler_params=pltpu.CompilerParams(
            collective_id=0, has_side_effects=True, vmem_limit_bytes=VMEM_LIMIT
        ),
        name="gradients",
    )(
        bucket_pos,
        bucket_len,
        mid_act,
        conv_cot,
        first_act,
        hidden_cot,
        upstream,
        out_act,
        weight_in,
        bucket,
        gain_in[None, :],
    )
    return tuple(outs)


def solution(mesh):
    return jax.shard_map(
        local,
        mesh=mesh,
        in_specs=(
            P(("dp", "shard"), None),
            P(),
            P(("dp", "shard")),
            P(("dp", "shard")),
            P(("dp", "shard")),
            P(("dp", "shard")),
            P(("dp", "shard")),
            P(("dp", "shard"), None),
            P(),
            P(),
            P(),
            P(),
            P(),
            P(),
        ),
        out_specs=(
            P(("dp", "shard"), None),
            P("dp", "shard"),
            P("dp", None, "shard"),
            P("dp", "shard"),
        ),
        check_vma=False,
    )
```

profile of v0, /device:TPU:0, one launch (start us, length us, event | category | flops | bytes accessed | tf_op | source)
XLA Modules:
  0.0 146.7 jit_solution(11358491726921360367)
XLA Ops:
  0.6 0.0 copy-start
  0.6 1.4 broadcast_in_dim.109.token
  2.1 48.0 %dispatch.1 = (bf16[384,1280]{1,0:T(8,128)(2,1)}, s32[384,1]{1,0:T(8,128)}, s32[384,1]{1,0:T(8,128)}) custom-call(s32[1,960]{1,0:T(1,128)} %bitcast.46, s32[1,960]{1,0:T(1,128)} %bitcast.47, s32[1,960]{1,0:T(1,128)} %bitcast.48, s32[1,960]{1,0:T(1,128)} %bitcast.49, bf16[1,1280]{1,0:T(2,128)(2,1)} %broadcast_in_dim.109.token, bf16[960,1280]{1,0:T(8,128)(2,1)} %embedded.1), custom_call_target="tpu_custom_call" | custom-call | tf_op jit(solution)/shard_map/dispatch/pallas_call | solution.py:452
  50.0 0.0 copy-start.3
  50.0 0.0 copy-start.6
  50.0 1.6 %convert_reduce_fusion = f32[384]{0:T(512)S(1)} fusion(bf16[384,1280]{1,0:T(8,128)(2,1)} %get-tuple-element.9.owner_input), kind=kLoop, calls=%fused_computation.2 | loop fusion | flops 982656 | bytes 984576 | tf_op jit(solution)/shard_map/reduce_sum | solution.py:18
  51.6 1.6 %fusion.2 = f32[384]{0:T(512)S(1)} fusion(bf16[384,1280]{1,0:T(8,128)(2,1)} %get-tuple-element.9.owner_input, f32[384]{0:T(512)S(1)} %broadcast_multiply_fusion.2), kind=kLoop, calls=%fused_computation.5 | loop fusion | flops 1965696 | bytes 986112 | tf_op jit(solution)/shard_map/reduce_sum | solution.py:20
  53.2 0.0 copy-done.12
  53.2 0.0 copy-done.3
  53.2 5.2 %fusion.7.first = bf16[384,1280]{1,0:T(8,128)(2,1)S(1)} fusion(bf16[384,1280]{1,0:T(8,128)(2,1)S(1)} %copy-done.3, f32[1280]{0:T(1024)S(1)} %copy-done.12, f32[384]{0:T(512)S(1)} %add_rsqrt_fusion, f32[384]{0:T(512)S(1)} %broadcast_multiply_fusion.2), kind=kLoop, calls=%fused_computation.10 | loop fusion | flops 33914880 | bytes 1974272 | tf_op jit(solution)/shard_map/convert_element_type | solution.py:60
  58.5 0.0 copy-done.6
  58.5 0.0 copy-start.5
  58.5 0.0 copy-start.14
  58.5 1.0 fusion.91
  59.5 0.0 copy-done.5
  59.5 0.0 copy-start.8
  59.6 0.0 copy-start.9
  59.6 0.0 copy-start.4
  59.6 0.3 multiply_reduce_fusion.3
  59.8 0.0 copy-done.14
  59.9 2.7 %multiply_convert_fusion.1.mid = bf16[384,640]{1,0:T(8,128)(2,1)S(1)} fusion(f32[384,640]{1,0:T(8,128)S(1)} %get-tuple-element.34, f32[640]{0:T(1024)S(1)} %copy-done.14, f32[384]{0:T(512)S(1)} %fusion.79, f32[384]{0:T(512)S(1)} %broadcast_multiply_fusion.1), kind=kLoop, calls=%fused_computation.64 | loop fusion | flops 16711680 | bytes 1480192 | tf_op jit(solution)/shard_map/convert_element_type | solution.py:63
  62.5 0.0 copy-start.1
  62.6 0.1 fusion.89
  62.6 0.0 copy-done.8
  62.6 0.0 copy-done.9
  62.7 0.4 and_reduce_fusion
  63.0 0.0 copy-done.4
  63.0 0.7 fusion.48
  63.7 0.1 fusion.90
  63.8 0.7 convolution_add_fusion.3
  64.4 0.0 copy-done.1
  64.4 0.7 convolution_add_fusion.2
  65.1 0.6 convolution_add_fusion.1
  65.7 0.0 copy-start.13
  65.8 0.8 fusion.92
  66.5 0.3 multiply_reduce_fusion.2
  66.8 0.0 copy-done.13
  66.8 3.4 %multiply_convert_fusion = (bf16[384,640]{1,0:T(8,128)(2,1)}, f32[384,640]{1,0:T(8,128)S(1)}) fusion(f32[384,640]{1,0:T(8,128)S(1)} %get-tuple-element.36, f32[640]{0:T(1024)S(1)} %copy-done.13, f32[384]{0:T(512)S(1)} %fusion.80, f32[384]{0:T(512)S(1)} %broadcast_multiply_fusion), kind=kLoop, calls=%fused_computation.43 | loop fusion | flops 16711680 | bytes 2463232 | tf_op jit(solution)/shard_map/convert_element_type | solution.py:88
  70.2 0.0 copy-done
  70.2 0.0 copy-done.7
  70.2 1.4 multiply_reduce_fusion.1
  71.6 1.0 fusion.88
  72.5 0.1 add_convert_fusion.1.conv_cot
  72.7 0.0 copy-start.2
  72.7 0.6 fusion.38
  73.3 0.6 fusion.43
  73.9 0.1 slice.63
  74.0 0.2 slice_select_fusion
  74.2 0.6 fusion.35
  74.8 0.6 fusion.46
  75.4 0.1 slice.61
  75.5 0.2 slice_select_fusion.2
  75.7 0.0 copy-done.2
  75.7 3.2 %multiply_reduce_fusion = (f32[384]{0:T(512)S(1)}, f32[384,640]{1,0:T(8,128)S(1)}) fusion(f32[384,640]{1,0:T(8,128)S(1)} %get-tuple-element.34, f32[384]{0:T(512)S(1)} %broadcast_multiply_fusion.1, f32[352,640]{1,0:T(8,128)S(1)} %get-tuple-element.43, f32[368,640]{1,0:T(8,128)S(1)} %get-tuple-element.41, ...), kind=kOutput, calls=%fused_computation.45 | convolution fusion | flops 334724736 | bytes 6973440 | tf_op jit(solution)/shard_map/dot_general | solution.py:41
  78.9 0.4 fusion.87
  79.3 0.9 add_convert_fusion.hidden_cot
  80.3 0.6 broadcast_in_dim.124.gain_in
  80.9 60.3 %gradients.1 = (bf16[384,1280]{1,0:T(8,128)(2,1)}, f32[160,160]{1,0:T(8,128)}, f32[80,5,160]{2,1,0:T(8,128)}, f32[160,160]{1,0:T(8,128)}) custom-call(s32[384,1]{1,0:T(8,128)} %get-tuple-element.7.position, s32[384,1]{1,0:T(8,128)} %get-tuple-element.8.length, bf16[384,640]{1,0:T(8,128)(2,1)} %copy-done.1, bf16[384,640]{1,0:T(8,128)(2,1)} %copy-done.2, ...), custom_call_target="tpu_custom_call" | custom-call | tf_op jit(solution)/shard_map/gradients/pallas_call | solution.py:499
  141.1 0.0 copy-start.11
  141.1 0.0 copy-start.10
  141.2 2.0 %copy.18 = f32[80,5,160]{2,0,1:T(8,128)} copy(f32[80,5,160]{2,1,0:T(8,128)} %get-tuple-element.16) | data formatting | bytes 512000 | tf_op jit(solution)/shard_map/gradients/pallas_call | solution.py:499
  143.2 2.2 %copy.22 = bf16[384,1280]{1,0:T(8,128)(2,1)} copy(bf16[384,1280]{1,0:T(8,128)(2,1)} %get-tuple-element.49) | data formatting | bytes 1966080
  145.4 0.7 copy.23
  146.1 0.7 copy.24
  (14 shorter events, 0.1 us)
Async XLA Ops:
  0.6 69.6 %copy-start = (bf16[1280,640]{1,0:T(8,128)(2,1)S(1)}, bf16[1280,640]{1,0:T(8,128)(2,1)}, u32[]{:S(2)}) copy-start(bf16[1280,640]{1,0:T(8,128)(2,1)} %param.26) | copy-start | bytes 4915204
  2.1 51.2 %copy-start.12 = (f32[1280]{0:T(1024)S(1)}, f32[1280]{0:T(1024)}, u32[]{:S(2)}) copy-start(f32[1280]{0:T(1024)} %param.21) | copy-start | bytes 15364
  50.0 3.2 %copy-start.3 = (bf16[384,1280]{1,0:T(8,128)(2,1)S(1)}, bf16[384,1280]{1,0:T(8,128)(2,1)}, u32[]{:S(2)}) copy-start(bf16[384,1280]{1,0:T(8,128)(2,1)} %get-tuple-element.9.owner_input) | copy-start | bytes 2949124
  50.0 8.5 %copy-start.6 = (bf16[1280,640]{1,0:T(8,128)(2,1)S(1)}, bf16[1280,640]{1,0:T(8,128)(2,1)}, u32[]{:S(2)}) copy-start(bf16[1280,640]{1,0:T(8,128)(2,1)} %weight_in.1) | copy-start | bytes 4915204
  58.5 1.0 copy-start.5
  58.5 1.3 copy-start.14
  59.5 3.1 %copy-start.8 = (s32[384,1]{1,0:T(8,128)S(1)}, s32[384,1]{1,0:T(8,128)}, u32[]{:S(2)}) copy-start(s32[384,1]{1,0:T(8,128)} %get-tuple-element.7.position) | copy-start | bytes 4612
  59.6 3.1 %copy-start.9 = (s32[384,1]{1,0:T(8,128)S(1)}, s32[384,1]{1,0:T(8,128)}, u32[]{:S(2)}) copy-start(s32[384,1]{1,0:T(8,128)} %get-tuple-element.8.length) | copy-start | bytes 4612
  59.6 3.5 %copy-start.4 = (bf16[640,5,640]{2,0,1:T(8,128)(2,1)S(1)}, bf16[640,5,640]{2,0,1:T(8,128)(2,1)}, u32[]{:S(2)}) copy-start(bf16[640,5,640]{2,0,1:T(8,128)(2,1)} %param.24) | copy-start | bytes 12288004
  62.5 1.9 %copy-start.1 = (bf16[384,640]{1,0:T(8,128)(2,1)}, bf16[384,640]{1,0:T(8,128)(2,1)S(1)}, u32[]{:S(2)}) copy-start(bf16[384,640]{1,0:T(8,128)(2,1)S(1)} %multiply_convert_fusion.1.mid) | copy-start | bytes 1474564
  65.7 1.1 copy-start.13
  66.5 3.7 %copy-start.7 = (bf16[384,1280]{1,0:T(8,128)(2,1)S(1)}, bf16[384,1280]{1,0:T(8,128)(2,1)}, u32[]{:S(2)}) copy-start(bf16[384,1280]{1,0:T(8,128)(2,1)} %upstream.1) | copy-start | bytes 2949124
  72.7 3.0 %copy-start.2 = (bf16[384,640]{1,0:T(8,128)(2,1)}, bf16[384,640]{1,0:T(8,128)(2,1)S(1)}, u32[]{:S(2)}) copy-start(bf16[384,640]{1,0:T(8,128)(2,1)S(1)} %add_convert_fusion.1.conv_cot) | copy-start | bytes 1474564
  141.1 4.2 %copy-start.11 = (f32[160,160]{1,0:T(8,128)S(1)}, f32[160,160]{1,0:T(8,128)}, u32[]{:S(2)}) copy-start(f32[160,160]{1,0:T(8,128)} %get-tuple-element.50) | copy-start | bytes 307204
  141.1 4.9 %copy-start.10 = (f32[160,160]{1,0:T(8,128)S(1)}, f32[160,160]{1,0:T(8,128)}, u32[]{:S(2)}) copy-start(f32[160,160]{1,0:T(8,128)} %get-tuple-element.52) | copy-start | bytes 307204
where the time goes:
time: 147 us
  Pallas kernels  108 us (73%)
  other arithmetic  18.2 us (12%)
  matrix products  11.4 us (8%)
  local copies, waits for them, and re-layouts  7.94 us (5%)
    pallas_call x1, Pallas kernels, local(): pl.pallas_call(functools.partial(gradient_kernel, owners, groups), out_sh...  60.3 us
    pallas_call x1, Pallas kernels, local(): pl.pallas_call(functools.partial(dispatch_kernel, owners), out_shape=[jax...  48 us
    dot_general x5, matrix products, contract_cols(): lax.dot_general(left, right, (((1,), (1,)), ((), ())), preferred_element_...  5.64 us
    convert_element_type x1, other arithmetic, layer_grads(): first_act = first_f32.astype(jnp.bfloat16)  5.24 us
    unnamed x33, local copies, waits for them, and re-layouts  3.62 us
    convert_element_type x1, other arithmetic, layer_grads(): out_act = out_f32.astype(jnp.bfloat16)  3.36 us

commit v1 on v0

v1 whole, which is shorter than its diff:
```python
import jax
import jax.numpy as jnp
from jax import lax
from jax.experimental import pallas as pl
from jax.experimental.pallas import tpu as pltpu
import functools
from jax.sharding import PartitionSpec as P

KERNEL_TAPS = 5
DILATION_STEP = 16
LMAX = 80


EPS = 1e-05


def raw_shift(values, offset):
    if offset > 0:
        filler = jnp.zeros((offset, values.shape[1]), values.dtype)
        return jnp.concatenate([values[offset:], filler], axis=0)
    if offset < 0:
        filler = jnp.zeros((-offset, values.shape[1]), values.dtype)
        return jnp.concatenate([filler, values[:offset]], axis=0)
    return values


def contract_rows(left, right):
    return lax.dot_general(
        left, right, (((0,), (0,)), ((), ())), preferred_element_type=jnp.float32
    )


def contract_cols(left, right):
    return lax.dot_general(
        left, right, (((1,), (1,)), ((), ())), preferred_element_type=jnp.float32
    )


MESH = pl.DeviceIdType.MESH


def bit_orders(owners, groups):
    dp_bits = [("dp", i) for i in range(owners.bit_length() - 1)]
    sh_bits = [("shard", i) for i in range(groups.bit_length() - 1)]
    first, others = sh_bits[:1], sh_bits[1:]
    return (
        first + others + dp_bits,
        first + dp_bits[:1] + others + dp_bits[1:],
        first + dp_bits[1:] + others + dp_bits[:1],
    )


def chunk_rows(rows):
    unit = rows // 5
    return (2 * unit, 2 * unit, unit)


def round_up(value, multiple):
    return -(-value // multiple) * multiple


def placed(values, offset):
    low = offset // 128 * 128
    high = round_up(offset + values.shape[1], 128)
    parts = []
    if offset > low:
        parts.append(jnp.zeros((values.shape[0], offset - low), values.dtype))
    parts.append(values)
    if high > offset + values.shape[1]:
        parts.append(jnp.zeros((values.shape[0], high - offset - values.shape[1]), values.dtype))
    return low, (jnp.concatenate(parts, axis=1) if len(parts) > 1 else values)


FILL = 64.0
INV_SQRT2 = 0.7071067811865476
INV_SQRT_2PI = 0.3989422804014327
VMEM_LIMIT = 60 * 1024 * 1024


def flipped(index, mask):
    other, bit = index, 0
    while (mask >> bit) > 0:
        if (mask >> bit) & 1:
            other = other + (1 - 2 * lax.rem(index // (1 << bit), 2)) * (1 << bit)
        bit += 1
    return other


def dispatch_kernel(
    owners,
    destination,
    position,
    order,
    timestep,
    token,
    embedded,
    bucket,
    bucket_pos,
    bucket_len,
    sent,
    got,
    send_sem,
    recv_sem,
):
    me, group = lax.axis_index("dp"), lax.axis_index("shard")
    barrier = pltpu.get_barrier_semaphore()
    for j in range(1, owners):
        pl.semaphore_signal(
            barrier, inc=1, device_id=(flipped(me, j), group), device_id_type=MESH
        )
    slot = jnp.where(destination[...] < owners, destination[...] * LMAX + position[...], -1)
    hidden_slot = (order[...] < timestep[...]).astype(jnp.float32)

    def block_for(owner):
        rows = lax.broadcasted_iota(jnp.int32, (LMAX, slot.shape[1]), 0) + owner * LMAX
        pick = (rows == slot).astype(jnp.float32)
        live = jnp.sum(pick, axis=1, keepdims=True)
        masked = jnp.sum(pick * hidden_slot, axis=1, keepdims=True)
        block = jnp.dot(
            pick.astype(jnp.bfloat16), embedded[...], preferred_element_type=jnp.float32
        )
        block = jnp.where(masked > 0.5, token[...].astype(jnp.float32), block)
        return jnp.where(live > 0.5, block, FILL).astype(jnp.bfloat16)

    copies = []
    for j in range(owners - 1, 0, -1):
        other = flipped(me, j)
        sent[j] = block_for(other)
        if j == owners - 1:
            pl.semaphore_wait(barrier, owners - 1)
        copy = pltpu.make_async_remote_copy(
            src_ref=sent.at[j],
            dst_ref=got.at[me],
            send_sem=send_sem.at[j],
            recv_sem=recv_sem.at[j],
            device_id=(other, group),
            device_id_type=MESH,
        )
        copy.start()
        copies.append(copy)
    got[me] = block_for(me)
    for copy in copies:
        copy.wait_recv()
    lanes = lax.broadcasted_iota(jnp.int32, (1, owners * LMAX), 1)
    place_of = jnp.full((1, owners * LMAX), -1, jnp.int32)
    pos_of = jnp.zeros((1, owners * LMAX), jnp.float32)
    len_of = jnp.zeros((1, owners * LMAX), jnp.float32)
    start = jnp.zeros((1, 1), jnp.int32)
    for source in range(owners):
        marks = got[source, :, 0:128].astype(jnp.float32)[:, 0:1]
        count = jnp.sum((marks < FILL / 2).astype(jnp.float32), axis=0, keepdims=True)
        whole = count.astype(jnp.int32)
        inside = lanes - source * LMAX
        used = (inside >= 0) & (inside < whole)
        place_of = jnp.where(used, start + inside, place_of)
        pos_of = jnp.where(used, inside.astype(jnp.float32), pos_of)
        len_of = jnp.where(used, count, len_of)
        start = start + whole
    own = bucket.shape[0]
    take = (
        lax.broadcasted_iota(jnp.int32, (own, owners * LMAX), 0) == place_of
    ).astype(jnp.float32)
    bucket_pos[...] = jnp.sum(take * pos_of, axis=1, keepdims=True).astype(jnp.int32)
    bucket_len[...] = jnp.sum(take * len_of, axis=1, keepdims=True).astype(jnp.int32)
    bucket[...] = jnp.dot(
        take.astype(jnp.bfloat16),
        got[...].reshape(owners * LMAX, bucket.shape[1]),
        preferred_element_type=jnp.float32,
    ).astype(jnp.bfloat16)
    for copy in copies:
        copy.wait_send()


def looped(rows, step, body):
    def run(i, carry):
        body(pl.ds(pl.multiple_of(i * step, step), step))
        return carry

    lax.fori_loop(0, rows // step, run, 0)


def normalize(value):
    centred = value - jnp.mean(value, axis=-1, keepdims=True)
    scale = lax.rsqrt(jnp.mean(centred * centred, axis=-1, keepdims=True) + EPS)
    return centred * scale, scale


def gelu_parts(scaled):
    half = 0.5 * (1.0 + lax.erf(scaled * INV_SQRT2))
    slope = half + scaled * (INV_SQRT_2PI * jnp.exp(-0.5 * scaled * scaled))
    return scaled * half, slope


def pull_back(cot, normal, scale):
    inner = jnp.mean(cot * normal, axis=-1, keepdims=True)
    return scale * (cot - jnp.mean(cot, axis=-1, keepdims=True) - normal * inner)


def part_layouts(narrow, wide):
    early = KERNEL_TAPS - 1
    return (
        ((0, early * narrow), (early * narrow, wide)),
        ((0, narrow), (narrow, wide)),
    )


def span_of(offset, size):
    return round_up(offset + size, 128) - offset // 128 * 128


def width_of(layout):
    return round_up(layout[-1][0] + layout[-1][1], 128)


def layer_kernel(
    owners,
    groups,
    position,
    length,
    owner_input,
    upstream,
    gain_in,
    gain_mid,
    gain_out,
    weight_in_hbm,
    weight_conv_hbm,
    weight_out_hbm,
    grad_input,
    grad_in,
    grad_conv,
    grad_out,
    *scratch,
):
    chunks = 3
    terms = (scratch[0:3], scratch[3:6])
    got = (scratch[6:9], scratch[9:12])
    left_conv, left_out, left_last, left_in = scratch[12:16]
    right_conv, right_out, right_in = scratch[16:19]
    weight_in, weight_conv, weight_out = scratch[19:22]
    first, mid, out_act, conv_cot, hidden_cot, taps = scratch[22:28]
    hidden, mid_gain, mid_scale, wide_a, wide_b = scratch[28:33]
    send_sem, recv_sem, load_sem = scratch[33:36]

    orders = bit_orders(owners, groups)
    steps = len(orders[0])
    total = 1 << steps
    me = {"dp": lax.axis_index("dp"), "shard": lax.axis_index("shard")}
    own_rows = owner_input.shape[0]
    narrow, wide = mid.shape[1] // owners, first.shape[1] // owners
    rows = right_conv.shape[0] // groups
    layouts = part_layouts(narrow, wide)

    def bit_of(axis, bit):
        return lax.rem(me[axis] // (1 << bit), 2)

    def partner(axis, bit):
        other = me[axis] + (1 - 2 * bit_of(axis, bit)) * (1 << bit)
        return (other, me["shard"]) if axis == "dp" else (me["dp"], other)

    loads = [
        pltpu.make_async_copy(source, target, load_sem.at[i])
        for i, (source, target) in enumerate(
            (
                (weight_out_hbm, weight_out),
                (weight_in_hbm, weight_in),
                (weight_conv_hbm, weight_conv),
            )
        )
    ]
    for load in loads:
        load.start()
    barrier = pltpu.get_barrier_semaphore()
    for axis, bit in orders[0]:
        pl.semaphore_signal(barrier, inc=1, device_id=partner(axis, bit), device_id_type=MESH)

    tap_offsets = [(k - KERNEL_TAPS // 2) * DILATION_STEP for k in range(KERNEL_TAPS)]

    def fill_taps(source, sign):
        for k, base_offset in enumerate(tap_offsets):
            offset = sign * base_offset
            moved = position[...] + offset
            valid = (moved >= 0) & (moved < length[...])
            shifted = raw_shift(source[...], offset)
            taps[k] = jnp.where(valid, shifted.astype(jnp.float32), 0.0).astype(jnp.bfloat16)

    def place(left, pieces, offset):
        for owner in range(owners):
            values = pieces(owner)
            left[owner] = placed(values, offset)[1].astype(jnp.bfloat16)

    def wide_piece(source):
        return lambda owner: source[:, owner * wide : (owner + 1) * wide].astype(jnp.float32)

    def half_terms(part, low_bit, sides):
        starts = [(2 * i + low_bit) * rows for i in range(groups // 2)]
        outs = terms[part]
        width = outs[0].shape[2]

        def body(owner, carry):
            tiles = [None] * (width // 128)
            for left, right, offset in sides:
                low = offset // 128
                picked = [right[pl.ds(pl.multiple_of(s, 16), rows), :] for s in starts]
                picked = picked[0] if len(picked) == 1 else jnp.concatenate(picked, axis=0)
                term = jnp.dot(picked, left[owner], preferred_element_type=jnp.float32)
                for j in range(left.shape[2] // 128):
                    piece = term[:, j * 128 : (j + 1) * 128]
                    held = tiles[low + j]
                    tiles[low + j] = piece if held is None else held + piece
            for j, tile in enumerate(tiles):
                tile = tile.astype(jnp.bfloat16)
                for i in range(groups // 2):
                    at = i * rows
                    for order, out in zip(orders, outs):
                        index = low_bit
                        for axis, bit in order[1:]:
                            if axis == "dp":
                                index = index * 2 + lax.rem(owner // (1 << bit), 2)
                            else:
                                index = index * 2 + (((2 * i) >> bit) & 1)
                        count = out.shape[1]
                        out[index, :, j * 128 : (j + 1) * 128] = tile[at : at + count]
                        at += count
            return carry

        lax.fori_loop(0, owners, body, 0)

    base, at = [], 0
    for t in range(steps):
        base.append(at)
        at += total >> (t + 1)

    def copy_of(part, c, t):
        half = total >> (t + 1)
        away = 1 - bit_of(*orders[c][t])
        source = terms[part][c] if t == 0 else got[part][c]
        start = away * half if t == 0 else base[t - 1] + away * half
        return pltpu.make_async_remote_copy(
            src_ref=source.at[pl.ds(start, half)],
            dst_ref=got[part][c].at[pl.ds(base[t], half)],
            send_sem=send_sem.at[part, c, t],
            recv_sem=recv_sem.at[part, c, t],
            device_id=partner(*orders[c][t]),
            device_id_type=MESH,
        )

    copies = [
        [[copy_of(part, c, t) for t in range(steps)] for c in range(chunks)] for part in range(2)
    ]

    def summed(part, c, t, at):
        half = total >> (t + 1)
        kept = bit_of(*orders[c][t]) * half
        source = terms[part][c] if t == 0 else got[part][c]
        offset = kept if t == 0 else base[t - 1] + kept
        here = got[part][c]
        return source[offset + at].astype(jnp.float32) + here[base[t] + at].astype(jnp.float32)

    def add(part, c, t, first_block, count):
        def body(i, carry):
            at = first_block + i
            got[part][c][base[t] + at] = summed(part, c, t, at).astype(jnp.bfloat16)
            return carry

        lax.fori_loop(0, count, body, 0)

    def advance(part, t):
        half = total >> (t + 2)
        for c in range(chunks):
            copies[part][c][t].wait_recv()
            nxt = bit_of(*orders[c][t + 1])
            add(part, c, t, (1 - nxt) * half, half)
            copies[part][c][t + 1].start()
        for c in range(chunks):
            nxt = bit_of(*orders[c][t + 1])
            add(part, c, t, nxt * half, half)

    def finish(part):
        finished = []
        for c in range(chunks):
            copies[part][c][steps - 1].wait_recv()
            finished.append(summed(part, c, steps - 1, 0))
        return jnp.concatenate(finished, axis=0).T

    place(left_out, wide_piece(upstream), layouts[0][1][0])
    loads[0].wait()
    wide_a[...] = jnp.dot(upstream[...], weight_out[...], preferred_element_type=jnp.float32)

    def first_rows(at):
        normal, _ = normalize(owner_input[at, :].astype(jnp.float32))
        first[at, :] = gelu_parts(normal * gain_in[...])[0].astype(jnp.bfloat16)

    looped(own_rows, 32, first_rows)
    loads[1].wait()
    hidden[...] = jnp.dot(first[...], weight_in[...], preferred_element_type=jnp.float32)

    def mid_rows(at):
        normal, scale = normalize(hidden[at, :])
        act, slope = gelu_parts(normal * gain_mid[...])
        mid[at, :] = act.astype(jnp.bfloat16)
        hidden[at, :] = normal
        mid_gain[at, :] = slope * gain_mid[...]
        mid_scale[at, :] = scale

    looped(own_rows, 32, mid_rows)
    fill_taps(mid, 1)
    loads[2].wait()
    conv = jnp.dot(taps[0], weight_conv[0], preferred_element_type=jnp.float32)
    for k in range(1, KERNEL_TAPS):
        conv = conv + jnp.dot(taps[k], weight_conv[k], preferred_element_type=jnp.float32)
    wide_b[...] = conv

    def out_rows(at):
        normal, scale = normalize(wide_b[at, :])
        act, slope = gelu_parts(normal * gain_out[...])
        out_act[at, :] = act.astype(jnp.bfloat16)
        cot = wide_a[at, :] * slope * gain_out[...]
        conv_cot[at, :] = pull_back(cot, normal, scale).astype(jnp.bfloat16)

    looped(own_rows, 32, out_rows)

    def tap_piece(ks):
        def piece(owner):
            here = slice(owner * narrow, (owner + 1) * narrow)
            parts = [taps[k, :, here].astype(jnp.float32) for k in ks]
            return parts[0] if len(parts) == 1 else jnp.concatenate(parts, axis=1)

        return piece

    place(left_conv, tap_piece(range(KERNEL_TAPS - 1)), layouts[0][0][0])
    right_conv[...] = conv_cot[...].T
    right_out[...] = out_act[...].T
    mine = bit_of(*orders[0][0])
    sides = (
        (
            (left_conv, right_conv, layouts[0][0][0]),
            (left_out, right_out, layouts[0][1][0]),
        ),
        (
            (left_last, right_conv, layouts[1][0][0]),
            (left_in, right_in, layouts[1][1][0]),
        ),
    )
    half_terms(0, 1 - mine, sides[0])
    pl.semaphore_wait(barrier, steps)
    for c in range(chunks):
        copies[0][c][0].start()
    half_terms(0, mine, sides[0])
    place(left_last, tap_piece((KERNEL_TAPS - 1,)), layouts[1][0][0])
    place(left_in, wide_piece(first), layouts[1][1][0])
    fill_taps(conv_cot, -1)
    advance(0, 0)
    mid_cot = contract_cols(taps[0], weight_conv[0])
    for k in range(1, KERNEL_TAPS):
        mid_cot = mid_cot + contract_cols(taps[k], weight_conv[k])
    wide_b[...] = mid_cot

    def hidden_rows(at):
        cot = wide_b[at, :] * mid_gain[at, :]
        hidden_cot[at, :] = pull_back(cot, hidden[at, :], mid_scale[at, :]).astype(jnp.bfloat16)

    looped(own_rows, 32, hidden_rows)
    right_in[...] = hidden_cot[...].T
    half_terms(1, 1 - mine, sides[1])
    for c in range(chunks):
        copies[1][c][0].start()
    half_terms(1, mine, sides[1])
    advance(0, 1)
    advance(1, 0)

    def input_rows(start):
        piece = jnp.concatenate([wide_a[start, :], wide_b[start, :]], axis=1)
        normal, scale = normalize(owner_input[start, :].astype(jnp.float32))
        slope = gelu_parts(normal * gain_in[...])[1]
        grad = pull_back(piece * slope * gain_in[...], normal, scale)
        grad_input[start, :] = (upstream[start, :].astype(jnp.float32) + grad).astype(
            jnp.bfloat16
        )

    halves = weight_in.shape[0] // 2
    wide_a[...] = contract_cols(hidden_cot[...], weight_in[:halves])
    wide_b[...] = contract_cols(hidden_cot[...], weight_in[halves:])
    looped(own_rows // 2, 32, input_rows)
    advance(0, 2)
    advance(1, 1)
    looped_from = own_rows // 2

    def late_rows(at):
        input_rows(pl.ds(pl.multiple_of(at.start + looped_from, 32), 32))

    looped(own_rows // 2, 32, late_rows)
    for t in range(3, steps):
        advance(0, t) if t < steps - 1 else None
        advance(1, t - 1)
    early = finish(0)
    for k in range(KERNEL_TAPS - 1):
        grad_conv[k] = early[k * narrow : (k + 1) * narrow]
    at = layouts[0][1][0]
    grad_out[...] = early[at : at + wide]
    late = finish(1)
    grad_conv[KERNEL_TAPS - 1] = late[:narrow]
    grad_in[...] = late[narrow : narrow + wide]
    for part in range(2):
        for c in range(chunks):
            for t in range(steps):
                copies[part][c][t].wait_send()


def local(
    embedded,
    mask_token_embedding,
    destination,
    position,
    length,
    unmask_order,
    timestep,
    upstream,
    gain_in,
    weight_in,
    gain_mid,
    weight_conv,
    gain_out,
    weight_out,
):
    channels = embedded.shape[1]
    owners, groups = lax.axis_size("dp"), lax.axis_size("shard")
    own_rows = upstream.shape[0]
    inner = weight_in.shape[1]
    vmem = pl.BlockSpec(memory_space=pltpu.VMEM)
    bucket, bucket_pos, bucket_len = pl.pallas_call(
        functools.partial(dispatch_kernel, owners),
        out_shape=[
            jax.ShapeDtypeStruct((own_rows, channels), jnp.bfloat16),
            jax.ShapeDtypeStruct((own_rows, 1), jnp.int32),
            jax.ShapeDtypeStruct((own_rows, 1), jnp.int32),
        ],
        in_specs=[vmem] * 6,
        out_specs=[vmem] * 3,
        scratch_shapes=[
            pltpu.VMEM((owners, LMAX, channels), jnp.bfloat16),
            pltpu.VMEM((owners, LMAX, channels), jnp.bfloat16),
            pltpu.SemaphoreType.DMA((owners,)),
            pltpu.SemaphoreType.DMA((owners,)),
        ],
        compiler_params=pltpu.CompilerParams(
            collective_id=1, has_side_effects=True, vmem_limit_bytes=VMEM_LIMIT
        ),
        name="dispatch",
    )(
        destination[None, :],
        position[None, :],
        unmask_order[None, :],
        timestep[None, :],
        mask_token_embedding[None, :],
        embedded,
    )
    narrow, wide, rows = inner // owners, channels // owners, inner // groups
    layouts = part_layouts(narrow, wide)
    total = owners * groups
    steps = total.bit_length() - 1
    counts = chunk_rows(rows)
    hbm = pl.BlockSpec(memory_space=pl.ANY)
    grad_input, grad_in, grad_conv, grad_out = pl.pallas_call(
        functools.partial(layer_kernel, owners, groups),
        out_shape=[
            jax.ShapeDtypeStruct((own_rows, channels), jnp.bfloat16),
            jax.ShapeDtypeStruct((wide, rows), jnp.float32),
            jax.ShapeDtypeStruct((KERNEL_TAPS, narrow, rows), jnp.float32),
            jax.ShapeDtypeStruct((wide, rows), jnp.float32),
        ],
        in_specs=[vmem] * 7 + [hbm] * 3,
        out_specs=[vmem] * 4,
        scratch_shapes=[
            pltpu.VMEM((total, n, width_of(layout)), jnp.bfloat16)
            for layout in layouts
            for n in counts
        ]
        + [
            pltpu.VMEM((total - 1, n, width_of(layout)), jnp.bfloat16)
            for layout in layouts
            for n in counts
        ]
        + [
            pltpu.VMEM((owners, own_rows, span_of(*item)), jnp.bfloat16)
            for layout in layouts
            for item in layout
        ]
        + [pltpu.VMEM((inner, own_rows), jnp.bfloat16)] * 3
        + [
            pltpu.VMEM((channels, inner), jnp.bfloat16),
            pltpu.VMEM((KERNEL_TAPS, inner, inner), jnp.bfloat16),
            pltpu.VMEM((channels, inner), jnp.bfloat16),
            pltpu.VMEM((own_rows, channels), jnp.bfloat16),
        ]
        + [pltpu.VMEM((own_rows, inner), jnp.bfloat16)] * 4
        + [pltpu.VMEM((KERNEL_TAPS, own_rows, inner), jnp.bfloat16)]
        + [
            pltpu.VMEM((own_rows, inner), jnp.float32),
            pltpu.VMEM((own_rows, inner), jnp.float32),
            pltpu.VMEM((own_rows, 1), jnp.float32),
            pltpu.VMEM((own_rows, inner), jnp.float32),
            pltpu.VMEM((own_rows, inner), jnp.float32),
        ]
        + [
            pltpu.SemaphoreType.DMA((2, 3, steps)),
            pltpu.SemaphoreType.DMA((2, 3, steps)),
            pltpu.SemaphoreType.DMA((3,)),
        ],
        compiler_params=pltpu.CompilerParams(
            collective_id=0, has_side_effects=True, vmem_limit_bytes=VMEM_LIMIT
        ),
        name="layer",
    )(
        bucket_pos,
        bucket_len,
        bucket,
        upstream,
        gain_in[None, :],
        gain_mid[None, :],
        gain_out[None, :],
        weight_in,
        jnp.transpose(weight_conv, (1, 0, 2)),
        weight_out,
    )
    return grad_input, grad_in, jnp.transpose(grad_conv, (1, 0, 2)), grad_out


def solution(mesh):
    return jax.shard_map(
        local,
        mesh=mesh,
        in_specs=(
            P(("dp", "shard"), None),
            P(),
            P(("dp", "shard")),
            P(("dp", "shard")),
            P(("dp", "shard")),
            P(("dp", "shard")),
            P(("dp", "shard")),
            P(("dp", "shard"), None),
            P(),
            P(),
            P(),
            P(),
            P(),
            P(),
        ),
        out_specs=(
            P(("dp", "shard"), None),
            P("dp", "shard"),
            P("dp", None, "shard"),
            P("dp", "shard"),
        ),
        check_vma=False,
    )
```

time: 147 us -> 127 us (0.86)
  other arithmetic: 18.2 us -> 0 us
  matrix products: 11.4 us -> 0 us
  Pallas kernels: 108 us -> 115 us
  local copies, waits for them, and re-layouts: 7.94 us -> 10.4 us
    convert_element_type x5 -> x0, other arithmetic: 12.3 us -> none  [the longest x1 5.24 us: layer_grads(): first_act = first_f32.astype(jnp.bfloat16)]
    dot_general x12 -> x0, matrix products: 11.4 us -> none  [the longest x5 5.64 us: contract_cols(): lax.dot_general(left, right, (((1,), (1,)), ((), ())), preferred_element_...]
    pallas_call x1, Pallas kernels: 60.3 us -> 67.1 us  [local(): pl.pallas_call(functools.partial(layer_kernel, owners, groups), out_shape...]
    reduce_sum x6 -> x0, other arithmetic: 5.04 us -> none  [the longest x3 2.11 us: normalized_activation(): row_var = jnp.mean(centred * centred, axis=-1, keepdims=True)]
    broadcast_in_dim x1 -> x3, local copies, waits for them, and re-layouts: 0.6 us -> 3.83 us  [the longest x1 1.29 us: local(): gain_in[None, :]]
    pallas_call x1 -> x0, local copies, waits for them, and re-layouts: 2.02 us -> none  [local(): pl.pallas_call(functools.partial(gradient_kernel, owners, groups), out_sh...]
    unnamed x33 -> x8, local copies, waits for them, and re-layouts: 3.62 us -> 5.29 us
where the time goes in v1:
time: 127 us; the launch traced here: 126 us
  Pallas kernels  115 us (91%)
  local copies, waits for them, and re-layouts  10.4 us (8%)
    pallas_call x1, Pallas kernels, local(): pl.pallas_call(functools.partial(layer_kernel, owners, groups), out_shape...  67.1 us
    pallas_call x1, Pallas kernels, local(): pl.pallas_call(functools.partial(dispatch_kernel, owners), out_shape=[jax...  48 us
    unnamed x8, local copies, waits for them, and re-layouts  5.29 us

profile of v1, /device:TPU:0, one launch (start us, length us, event | category | flops | bytes accessed | tf_op | source)
XLA Modules:
  0.0 126.2 jit_solution(16455268883608910419)
XLA Ops:
  0.6 1.3 %broadcast_in_dim.30.gain_mid = f32[1,640]{1,0:T(1,128)} reshape(f32[640]{0:T(1024)} %param.23) | data formatting | bytes 5120 | tf_op jit(solution)/shard_map/broadcast_in_dim | solution.py:619
  1.9 1.3 %broadcast_in_dim.31.gain_out = f32[1,640]{1,0:T(1,128)} reshape(f32[640]{0:T(1024)} %param.25) | data formatting | bytes 5120 | tf_op jit(solution)/shard_map/broadcast_in_dim | solution.py:620
  3.2 1.3 %broadcast_in_dim.28.token = bf16[1,1280]{1,0:T(2,128)(2,1)} reshape(bf16[1280]{0:T(1024)(128)(2,1)} %param.15) | data formatting | bytes 5120 | tf_op jit(solution)/shard_map/broadcast_in_dim | solution.py:554
  4.4 1.3 %broadcast_in_dim.29.gain_in = f32[1,1280]{1,0:T(1,128)} reshape(f32[1280]{0:T(1024)} %param.21) | data formatting | bytes 10240 | tf_op jit(solution)/shard_map/broadcast_in_dim | solution.py:618
  5.7 48.0 %dispatch.1 = (bf16[384,1280]{1,0:T(8,128)(2,1)}, s32[384,1]{1,0:T(8,128)}, s32[384,1]{1,0:T(8,128)}) custom-call(s32[1,960]{1,0:T(1,128)} %bitcast.8, s32[1,960]{1,0:T(1,128)} %bitcast.9, s32[1,960]{1,0:T(1,128)} %bitcast.10, s32[1,960]{1,0:T(1,128)} %bitcast.11, bf16[1,1280]{1,0:T(2,128)(2,1)} %broadcast_in_dim.28.token, bf16[960,1280]{1,0:T(8,128)(2,1)} %embedded.1), custom_call_target="tpu_custom_call" | custom-call | tf_op jit(solution)/shard_map/dispatch/pallas_call | solution.py:530
  53.8 67.1 %layer.1 = (bf16[384,1280]{1,0:T(8,128)(2,1)}, f32[160,160]{1,0:T(8,128)}, f32[5,80,160]{2,1,0:T(8,128)}, f32[160,160]{1,0:T(8,128)}) custom-call(s32[384,1]{1,0:T(8,128)} %get-tuple-element.11.position, s32[384,1]{1,0:T(8,128)} %get-tuple-element.12.length, bf16[384,1280]{1,0:T(8,128)(2,1)} %get-tuple-element.13.owner_input, bf16[384,1280]{1,0:T(8,128)(2,1)} %upstream.1, ...), custom_call_target="tpu_custom_call" | custom-call | tf_op jit(solution)/shard_map/layer/pallas_call | solution.py:563
  120.9 0.0 copy-start
  120.9 0.0 copy-start.1
  120.9 2.3 %copy.21 = bf16[384,1280]{1,0:T(8,128)(2,1)} copy(bf16[384,1280]{1,0:T(8,128)(2,1)} %get-tuple-element.22) | data formatting | bytes 1966080
  123.2 1.6 %copy.22 = f32[160,160]{1,0:T(8,128)} copy(f32[160,160]{1,0:T(8,128)} %get-tuple-element.23) | data formatting | bytes 204800
  124.8 0.0 copy-done
  124.8 0.8 copy.23
  125.5 0.0 copy-done.1
  125.6 0.7 copy.24
Async XLA Ops:
  120.9 3.9 %copy-start = (f32[5,80,160]{2,1,0:T(8,128)S(1)}, f32[5,80,160]{2,1,0:T(8,128)}, u32[]{:S(2)}) copy-start(f32[5,80,160]{2,1,0:T(8,128)} %get-tuple-element.16) | copy-start | bytes 768004
  120.9 4.6 %copy-start.1 = (f32[160,160]{1,0:T(8,128)S(1)}, f32[160,160]{1,0:T(8,128)}, u32[]{:S(2)}) copy-start(f32[160,160]{1,0:T(8,128)} %get-tuple-element.25) | copy-start | bytes 307204

commit v2 on v1

--- a/solution.py
+++ b/solution.py
@@ -41,12 +41,11 @@
 
 def bit_orders(owners, groups):
     dp_bits = [("dp", i) for i in range(owners.bit_length() - 1)]
-    sh_bits = [("shard", i) for i in range(groups.bit_length() - 1)]
-    first, others = sh_bits[:1], sh_bits[1:]
+    chip_bits = [("shard", i) for i in range(1, groups.bit_length() - 1)]
     return (
-        first + others + dp_bits,
-        first + dp_bits[:1] + others + dp_bits[1:],
-        first + dp_bits[1:] + others + dp_bits[:1],
+        chip_bits + dp_bits,
+        dp_bits[:1] + chip_bits + dp_bits[1:],
+        dp_bits[1:] + chip_bits + dp_bits[:1],
     )
 
 
@@ -119,7 +118,7 @@
         block = jnp.dot(
             pick.astype(jnp.bfloat16), embedded[...], preferred_element_type=jnp.float32
         )
-        block = jnp.where(masked > 0.5, token[...].astype(jnp.float32), block)
+        block = jnp.where(masked > 0.5, token[...][None, :].astype(jnp.float32), block)
         return jnp.where(live > 0.5, block, FILL).astype(jnp.bfloat16)
 
     copies = []
@@ -226,9 +225,8 @@
     weight_conv_hbm,
     weight_out_hbm,
     grad_input,
-    grad_in,
-    grad_conv,
-    grad_out,
+    early_sum,
+    late_sum,
     *scratch,
 ):
     chunks = 3
@@ -239,7 +237,8 @@
     weight_in, weight_conv, weight_out = scratch[19:22]
     first, mid, out_act, conv_cot, hidden_cot, taps = scratch[22:28]
     hidden, mid_gain, mid_scale, wide_a, wide_b = scratch[28:33]
-    send_sem, recv_sem, load_sem = scratch[33:36]
+    right_conv_peer, right_out_peer, right_in_peer = scratch[33:36]
+    send_sem, recv_sem, load_sem, factor_send, factor_recv = scratch[36:41]
 
     orders = bit_orders(owners, groups)
     steps = len(orders[0])
@@ -247,7 +246,7 @@
     me = {"dp": lax.axis_index("dp"), "shard": lax.axis_index("shard")}
     own_rows = owner_input.shape[0]
     narrow, wide = mid.shape[1] // owners, first.shape[1] // owners
-    rows = right_conv.shape[0] // groups
+    rows = right_conv.shape[2]
     layouts = part_layouts(narrow, wide)
 
     def bit_of(axis, bit):
@@ -270,8 +269,31 @@
     for load in loads:
         load.start()
     barrier = pltpu.get_barrier_semaphore()
-    for axis, bit in orders[0]:
+    for axis, bit in [("shard", 0)] + orders[0]:
         pl.semaphore_signal(barrier, inc=1, device_id=partner(axis, bit), device_id_type=MESH)
+    core = bit_of("shard", 0)
+
+    def to_other_core(number, source, target):
+        return pltpu.make_async_remote_copy(
+            src_ref=source,
+            dst_ref=target,
+            send_sem=factor_send.at[number],
+            recv_sem=factor_recv.at[number],
+            device_id=partner("shard", 0),
+            device_id_type=MESH,
+        )
+
+    lefts = (left_conv, left_out, left_last, left_in)
+    left_copies = [to_other_core(n, ref.at[0], ref.at[1]) for n, ref in enumerate(lefts)]
+    rights = ((right_conv, right_conv_peer), (right_out, right_out_peer), (right_in, right_in_peer))
+    right_copies = [
+        to_other_core(4 + n, ref.at[1 - core], peer) for n, (ref, peer) in enumerate(rights)
+    ]
+
+    def turn(right, values):
+        turned = values[...].T
+        for g in range(groups):
+            right[g % 2, g // 2] = turned[g * rows : (g + 1) * rows]
 
     tap_offsets = [(k - KERNEL_TAPS // 2) * DILATION_STEP for k in range(KERNEL_TAPS)]
 
@@ -286,24 +308,30 @@
     def place(left, pieces, offset):
         for owner in range(owners):
             values = pieces(owner)
-            left[owner] = placed(values, offset)[1].astype(jnp.bfloat16)
+            left[0, owner] = placed(values, offset)[1].astype(jnp.bfloat16)
 
     def wide_piece(source):
         return lambda owner: source[:, owner * wide : (owner + 1) * wide].astype(jnp.float32)
 
-    def half_terms(part, low_bit, sides):
-        starts = [(2 * i + low_bit) * rows for i in range(groups // 2)]
+    def multiply(part, low_bit, sides):
         outs = terms[part]
         width = outs[0].shape[2]
 
-        def body(owner, carry):
+        def body(pair, carry):
+            owner = pair * 2 + low_bit
             tiles = [None] * (width // 128)
-            for left, right, offset in sides:
+            for left, (right, peer), offset in sides:
                 low = offset // 128
-                picked = [right[pl.ds(pl.multiple_of(s, 16), rows), :] for s in starts]
-                picked = picked[0] if len(picked) == 1 else jnp.concatenate(picked, axis=0)
-                term = jnp.dot(picked, left[owner], preferred_element_type=jnp.float32)
-                for j in range(left.shape[2] // 128):
+                picked = jnp.concatenate(
+                    [
+                        right[core].reshape(groups // 2 * rows, own_rows),
+                        peer[...].reshape(groups // 2 * rows, own_rows),
+                    ],
+                    axis=1,
+                )
+                both = jnp.concatenate([left[0, owner], left[1, owner]], axis=0)
+                term = jnp.dot(picked, both, preferred_element_type=jnp.float32)
+                for j in range(left.shape[3] // 128):
                     piece = term[:, j * 128 : (j + 1) * 128]
                     held = tiles[low + j]
                     tiles[low + j] = piece if held is None else held + piece
@@ -312,18 +340,18 @@
                 for i in range(groups // 2):
                     at = i * rows
                     for order, out in zip(orders, outs):
-                        index = low_bit
-                        for axis, bit in order[1:]:
+                        index = 0
+                        for axis, bit in order:
                             if axis == "dp":
                                 index = index * 2 + lax.rem(owner // (1 << bit), 2)
                             else:
-                                index = index * 2 + (((2 * i) >> bit) & 1)
+                                index = index * 2 + ((i >> (bit - 1)) & 1)
                         count = out.shape[1]
                         out[index, :, j * 128 : (j + 1) * 128] = tile[at : at + count]
                         at += count
             return carry
 
-        lax.fori_loop(0, owners, body, 0)
+        lax.fori_loop(0, owners // 2, body, 0)
 
     base, at = [], 0
     for t in range(steps):
@@ -380,7 +408,15 @@
         for c in range(chunks):
             copies[part][c][steps - 1].wait_recv()
             finished.append(summed(part, c, steps - 1, 0))
-        return jnp.concatenate(finished, axis=0).T
+        return jnp.concatenate(finished, axis=0)
+
+    def tap_piece(ks):
+        def piece(owner):
+            here = slice(owner * narrow, (owner + 1) * narrow)
+            parts = [taps[k, :, here].astype(jnp.float32) for k in ks]
+            return parts[0] if len(parts) == 1 else jnp.concatenate(parts, axis=1)
+
+        return piece
 
     place(left_out, wide_piece(upstream), layouts[0][1][0])
     loads[0].wait()
@@ -388,7 +424,7 @@
 
     def first_rows(at):
         normal, _ = normalize(owner_input[at, :].astype(jnp.float32))
-        first[at, :] = gelu_parts(normal * gain_in[...])[0].astype(jnp.bfloat16)
+        first[at, :] = gelu_parts(normal * gain_in[...][None, :])[0].astype(jnp.bfloat16)
 
     looped(own_rows, 32, first_rows)
     loads[1].wait()
@@ -396,14 +432,20 @@
 
     def mid_rows(at):
         normal, scale = normalize(hidden[at, :])
-        act, slope = gelu_parts(normal * gain_mid[...])
+        act, slope = gelu_parts(normal * gain_mid[...][None, :])
         mid[at, :] = act.astype(jnp.bfloat16)
         hidden[at, :] = normal
-        mid_gain[at, :] = slope * gain_mid[...]
+        mid_gain[at, :] = slope * gain_mid[...][None, :]
         mid_scale[at, :] = scale
 
     looped(own_rows, 32, mid_rows)
     fill_taps(mid, 1)
+    pl.semaphore_wait(barrier, steps + 1)
+    left_copies[1].start()
+    place(left_conv, tap_piece(range(KERNEL_TAPS - 1)), layouts[0][0][0])
+    left_copies[0].start()
+    place(left_last, tap_piece((KERNEL_TAPS - 1,)), layouts[1][0][0])
+    left_copies[2].start()
     loads[2].wait()
     conv = jnp.dot(taps[0], weight_conv[0], preferred_element_type=jnp.float32)
     for k in range(1, KERNEL_TAPS):
@@ -412,44 +454,39 @@
 
     def out_rows(at):
         normal, scale = normalize(wide_b[at, :])
-        act, slope = gelu_parts(normal * gain_out[...])
+        act, slope = gelu_parts(normal * gain_out[...][None, :])
         out_act[at, :] = act.astype(jnp.bfloat16)
-        cot = wide_a[at, :] * slope * gain_out[...]
+        cot = wide_a[at, :] * slope * gain_out[...][None, :]
         conv_cot[at, :] = pull_back(cot, normal, scale).astype(jnp.bfloat16)
 
     looped(own_rows, 32, out_rows)
-
-    def tap_piece(ks):
-        def piece(owner):
-            here = slice(owner * narrow, (owner + 1) * narrow)
-            parts = [taps[k, :, here].astype(jnp.float32) for k in ks]
-            return parts[0] if len(parts) == 1 else jnp.concatenate(parts, axis=1)
-
-        return piece
-
-    place(left_conv, tap_piece(range(KERNEL_TAPS - 1)), layouts[0][0][0])
-    right_conv[...] = conv_cot[...].T
-    right_out[...] = out_act[...].T
-    mine = bit_of(*orders[0][0])
+    turn(right_conv, conv_cot)
+    right_copies[0].start()
+    turn(right_out, out_act)
+    right_copies[1].start()
+    fill_taps(conv_cot, -1)
+    place(left_in, wide_piece(first), layouts[1][1][0])
+    left_copies[3].start()
+    side_bit = bit_of(*orders[1][0])
     sides = (
         (
-            (left_conv, right_conv, layouts[0][0][0]),
-            (left_out, right_out, layouts[0][1][0]),
+            (left_conv, rights[0], layouts[0][0][0]),
+            (left_out, rights[1], layouts[0][1][0]),
         ),
         (
-            (left_last, right_conv, layouts[1][0][0]),
-            (left_in, right_in, layouts[1][1][0]),
+            (left_last, rights[0], layouts[1][0][0]),
+            (left_in, rights[2], layouts[1][1][0]),
         ),
     )
-    half_terms(0, 1 - mine, sides[0])
-    pl.semaphore_wait(barrier, steps)
-    for c in range(chunks):
-        copies[0][c][0].start()
-    half_terms(0, mine, sides[0])
-    place(left_last, tap_piece((KERNEL_TAPS - 1,)), layouts[1][0][0])
-    place(left_in, wide_piece(first), layouts[1][1][0])
-    fill_taps(conv_cot, -1)
-    advance(0, 0)
+    left_copies[1].wait_recv()
+    left_copies[0].wait_recv()
+    right_copies[0].wait_recv()
+    right_copies[1].wait_recv()
+    multiply(0, 1 - side_bit, sides[0])
+    copies[0][1][0].start()
+    multiply(0, side_bit, sides[0])
+    copies[0][0][0].start()
+    copies[0][2][0].start()
     mid_cot = contract_cols(taps[0], weight_conv[0])
     for k in range(1, KERNEL_TAPS):
         mid_cot = mid_cot + contract_cols(taps[k], weight_conv[k])
@@ -460,50 +497,64 @@
         hidden_cot[at, :] = pull_back(cot, hidden[at, :], mid_scale[at, :]).astype(jnp.bfloat16)
 
     looped(own_rows, 32, hidden_rows)
-    right_in[...] = hidden_cot[...].T
-    half_terms(1, 1 - mine, sides[1])
-    for c in range(chunks):
-        copies[1][c][0].start()
-    half_terms(1, mine, sides[1])
-    advance(0, 1)
-    advance(1, 0)
+    turn(right_in, hidden_cot)
+    right_copies[2].start()
+    halves = weight_in.shape[0] // 2
+    wide_a[...] = contract_cols(hidden_cot[...], weight_in[:halves])
+    left_copies[2].wait_recv()
+    left_copies[3].wait_recv()
+    right_copies[2].wait_recv()
+    multiply(1, 1 - side_bit, sides[1])
+    copies[1][1][0].start()
+    multiply(1, side_bit, sides[1])
+    copies[1][0][0].start()
+    copies[1][2][0].start()
+    wide_b[...] = contract_cols(hidden_cot[...], weight_in[halves:])
 
     def input_rows(start):
         piece = jnp.concatenate([wide_a[start, :], wide_b[start, :]], axis=1)
         normal, scale = normalize(owner_input[start, :].astype(jnp.float32))
-        slope = gelu_parts(normal * gain_in[...])[1]
-        grad = pull_back(piece * slope * gain_in[...], normal, scale)
+        slope = gelu_parts(normal * gain_in[...][None, :])[1]
+        grad = pull_back(piece * slope * gain_in[...][None, :], normal, scale)
         grad_input[start, :] = (upstream[start, :].astype(jnp.float32) + grad).astype(
             jnp.bfloat16
         )
 
-    halves = weight_in.shape[0] // 2
-    wide_a[...] = contract_cols(hidden_cot[...], weight_in[:halves])
-    wide_b[...] = contract_cols(hidden_cot[...], weight_in[halves:])
+    def late_rows(at):
+        input_rows(pl.ds(pl.multiple_of(at.start + own_rows // 2, 32), 32))
+
+    advance(0, 0)
     looped(own_rows // 2, 32, input_rows)
-    advance(0, 2)
-    advance(1, 1)
-    looped_from = own_rows // 2
-
-    def late_rows(at):
-        input_rows(pl.ds(pl.multiple_of(at.start + looped_from, 32), 32))
-
+    advance(0, 1)
+    advance(1, 0)
     looped(own_rows // 2, 32, late_rows)
-    for t in range(3, steps):
-        advance(0, t) if t < steps - 1 else None
+    for t in range(2, steps):
+        if t < steps - 1:
+            advance(0, t)
         advance(1, t - 1)
-    early = finish(0)
-    for k in range(KERNEL_TAPS - 1):
-        grad_conv[k] = early[k * narrow : (k + 1) * narrow]
-    at = layouts[0][1][0]
-    grad_out[...] = early[at : at + wide]
-    late = finish(1)
-    grad_conv[KERNEL_TAPS - 1] = late[:narrow]
-    grad_in[...] = late[narrow : narrow + wide]
+    early_sum[...] = finish(0)
+    late_sum[...] = finish(1)
+    for copy in left_copies + right_copies:
+        copy.wait_send()
     for part in range(2):
         for c in range(chunks):
             for t in range(steps):
                 copies[part][c][t].wait_send()
+
+
+def result_kernel(
+    layouts, grad_rows, early_sum, late_sum, grad_input, grad_in, grad_conv, grad_out
+):
+    grad_input[...] = grad_rows[...]
+    narrow, wide = grad_conv.shape[1], grad_in.shape[0]
+    early, late = early_sum[...].T, late_sum[...].T
+    for k in range(KERNEL_TAPS - 1):
+        grad_conv[k] = early[k * narrow : (k + 1) * narrow]
+    grad_conv[KERNEL_TAPS - 1] = late[:narrow]
+    at = layouts[0][1][0]
+    grad_out[...] = early[at : at + wide]
+    at = layouts[1][1][0]
+    grad_in[...] = late[at : at + wide]
 
 
 def local(
@@ -551,25 +602,21 @@
         position[None, :],
         unmask_order[None, :],
         timestep[None, :],
-        mask_token_embedding[None, :],
+        mask_token_embedding,
         embedded,
     )
     narrow, wide, rows = inner // owners, channels // owners, inner // groups
     layouts = part_layouts(narrow, wide)
-    total = owners * groups
+    total = owners * groups // 2
     steps = total.bit_length() - 1
     counts = chunk_rows(rows)
     hbm = pl.BlockSpec(memory_space=pl.ANY)
-    grad_input, grad_in, grad_conv, grad_out = pl.pallas_call(
+    partial_results = pl.pallas_call(
         functools.partial(layer_kernel, owners, groups),
-        out_shape=[
-            jax.ShapeDtypeStruct((own_rows, channels), jnp.bfloat16),
-            jax.ShapeDtypeStruct((wide, rows), jnp.float32),
-            jax.ShapeDtypeStruct((KERNEL_TAPS, narrow, rows), jnp.float32),
-            jax.ShapeDtypeStruct((wide, rows), jnp.float32),
-        ],
+        out_shape=[jax.ShapeDtypeStruct((own_rows, channels), jnp.bfloat16)]
+        + [jax.ShapeDtypeStruct((rows, width_of(layout)), jnp.float32) for layout in layouts],
         in_specs=[vmem] * 7 + [hbm] * 3,
-        out_specs=[vmem] * 4,
+        out_specs=[vmem] * 3,
         scratch_shapes=[
             pltpu.VMEM((total, n, width_of(layout)), jnp.bfloat16)
             for layout in layouts
@@ -581,11 +628,11 @@
             for n in counts
         ]
         + [
-            pltpu.VMEM((owners, own_rows, span_of(*item)), jnp.bfloat16)
+            pltpu.VMEM((2, owners, own_rows, span_of(*item)), jnp.bfloat16)
             for layout in layouts
             for item in layout
         ]
-        + [pltpu.VMEM((inner, own_rows), jnp.bfloat16)] * 3
+        + [pltpu.VMEM((2, groups // 2, rows, own_rows), jnp.bfloat16)] * 3
         + [
             pltpu.VMEM((channels, inner), jnp.bfloat16),
             pltpu.VMEM((KERNEL_TAPS, inner, inner), jnp.bfloat16),
@@ -601,10 +648,13 @@
             pltpu.VMEM((own_rows, inner), jnp.float32),
             pltpu.VMEM((own_rows, inner), jnp.float32),
         ]
+        + [pltpu.VMEM((groups // 2, rows, own_rows), jnp.bfloat16)] * 3
         + [
             pltpu.SemaphoreType.DMA((2, 3, steps)),
             pltpu.SemaphoreType.DMA((2, 3, steps)),
             pltpu.SemaphoreType.DMA((3,)),
+            pltpu.SemaphoreType.DMA((7,)),
+            pltpu.SemaphoreType.DMA((7,)),
         ],
         compiler_params=pltpu.CompilerParams(
             collective_id=0, has_side_effects=True, vmem_limit_bytes=VMEM_LIMIT
@@ -615,13 +665,25 @@
         bucket_len,
         bucket,
         upstream,
-        gain_in[None, :],
-        gain_mid[None, :],
-        gain_out[None, :],
+        gain_in,
+        gain_mid,
+        gain_out,
         weight_in,
         jnp.transpose(weight_conv, (1, 0, 2)),
         weight_out,
     )
+    grad_input, grad_in, grad_conv, grad_out = pl.pallas_call(
+        functools.partial(result_kernel, layouts),
+        out_shape=[
+            jax.ShapeDtypeStruct((own_rows, channels), jnp.bfloat16),
+            jax.ShapeDtypeStruct((wide, rows), jnp.float32),
+            jax.ShapeDtypeStruct((KERNEL_TAPS, narrow, rows), jnp.float32),
+            jax.ShapeDtypeStruct((wide, rows), jnp.float32),
+        ],
+        in_specs=[vmem] * 3,
+        out_specs=[vmem] * 4,
+        name="results",
+    )(*partial_results)
     return grad_input, grad_in, jnp.transpose(grad_conv, (1, 0, 2)), grad_out
 
 

time: 127 us -> 119 us (0.937)
  local copies, waits for them, and re-layouts: 10.4 us -> 0 us
  Pallas kernels: 115 us -> 119 us
    unnamed x8 -> x0, local copies, waits for them, and re-layouts: 5.29 us -> none
    broadcast_in_dim x4 -> x0, local copies, waits for them, and re-layouts: 5.11 us -> none  [the longest x1 1.29 us: local(): gain_in[None, :]]
    pallas_call x0 -> x1, Pallas kernels: none -> 2.7 us  [local(): pl.pallas_call(functools.partial(result_kernel, layouts), out_shape=[jax....]
where the time goes in v2:
time: 119 us
  Pallas kernels  119 us (100%)
    pallas_call x1, Pallas kernels, local(): pl.pallas_call(functools.partial(layer_kernel, owners, groups), out_shape...  67.9 us
    pallas_call x1, Pallas kernels, local(): pl.pallas_call(functools.partial(dispatch_kernel, owners), out_shape=[jax...  48 us
    pallas_call x1, Pallas kernels, local(): pl.pallas_call(functools.partial(result_kernel, layouts), out_shape=[jax....  2.7 us

profile of v2, /device:TPU:0, one launch (start us, length us, event | category | flops | bytes accessed | tf_op | source)
XLA Modules:
  0.0 119.2 jit_solution(6541541574203552041)
XLA Ops:
  0.6 48.0 %dispatch.1 = (bf16[384,1280]{1,0:T(8,128)(2,1)}, s32[384,1]{1,0:T(8,128)}, s32[384,1]{1,0:T(8,128)}) custom-call(s32[1,960]{1,0:T(1,128)} %bitcast.7, s32[1,960]{1,0:T(1,128)} %bitcast.8, s32[1,960]{1,0:T(1,128)} %bitcast.9, s32[1,960]{1,0:T(1,128)} %bitcast.10, bf16[1280]{0:T(1024)(128)(2,1)} %token_.1, bf16[960,1280]{1,0:T(8,128)(2,1)} %embedded.1), custom_call_target="tpu_custom_call" | custom-call | tf_op jit(solution)/shard_map/dispatch/pallas_call | solution.py:581
  48.6 67.9 %layer.1 = (bf16[384,1280]{1,0:T(8,128)(2,1)}, f32[160,512]{1,0:T(8,128)}, f32[160,256]{1,0:T(8,128)}) custom-call(s32[384,1]{1,0:T(8,128)} %get-tuple-element.14.position, s32[384,1]{1,0:T(8,128)} %get-tuple-element.15.length, bf16[384,1280]{1,0:T(8,128)(2,1)} %get-tuple-element.16.owner_input, bf16[384,1280]{1,0:T(8,128)(2,1)} %upstream.1, f32[1280]{0:T(1024)} %gain_in.1, ...), custom_call_target="tpu_custom_call" | custom-call | tf_op jit(solution)/shard_map/layer/pallas_call | solution.py:614
  116.5 2.7 %results.1 = (bf16[384,1280]{1,0:T(8,128)(2,1)}, f32[160,160]{1,0:T(8,128)}, f32[5,80,160]{2,1,0:T(8,128)}, f32[160,160]{1,0:T(8,128)}) custom-call(bf16[384,1280]{1,0:T(8,128)(2,1)} %get-tuple-element.17.grad_rows, f32[160,512]{1,0:T(8,128)} %get-tuple-element.18.early_sum, f32[160,256]{1,0:T(8,128)} %get-tuple-element.19.late_sum), custom_call_target="tpu_custom_call" | custom-call | tf_op jit(solution)/shard_map/results/pallas_call | solution.py:675

commit v3 on v2

--- a/solution.py
+++ b/solution.py
@@ -74,6 +74,7 @@
 INV_SQRT2 = 0.7071067811865476
 INV_SQRT_2PI = 0.3989422804014327
 VMEM_LIMIT = 60 * 1024 * 1024
+BLOCK_LIMIT = 8 * 1024 * 1024
 
 
 def flipped(index, mask):
@@ -83,6 +84,48 @@
             other = other + (1 - 2 * lax.rem(index // (1 << bit), 2)) * (1 << bit)
         bit += 1
     return other
+
+
+def block_builder(owners, destination, place, order, timestep, token, embedded):
+    slot = jnp.where(destination[...] < owners, destination[...] * LMAX + place[...], -1)
+    hidden_slot = (order[...] < timestep[...]).astype(jnp.float32)
+
+    def block_for(owner):
+        rows = lax.broadcasted_iota(jnp.int32, (LMAX, slot.shape[1]), 0) + owner * LMAX
+        pick = (rows == slot).astype(jnp.float32)
+        live = jnp.sum(pick, axis=1, keepdims=True)
+        masked = jnp.sum(pick * hidden_slot, axis=1, keepdims=True)
+        block = jnp.dot(
+            pick.astype(jnp.bfloat16), embedded[...], preferred_element_type=jnp.float32
+        )
+        block = jnp.where(masked > 0.5, token[...][None, :].astype(jnp.float32), block)
+        return jnp.where(live > 0.5, block, FILL).astype(jnp.bfloat16)
+
+    return block_for
+
+
+def ordering(owners, own, got):
+    lanes = lax.broadcasted_iota(jnp.int32, (1, owners * LMAX), 1)
+    place_of = jnp.full((1, owners * LMAX), -1, jnp.int32)
+    pos_of = jnp.zeros((1, owners * LMAX), jnp.float32)
+    len_of = jnp.zeros((1, owners * LMAX), jnp.float32)
+    start = jnp.zeros((1, 1), jnp.int32)
+    for source in range(owners):
+        marks = got[source, :, 0:128].astype(jnp.float32)[:, 0:1]
+        count = jnp.sum((marks < FILL / 2).astype(jnp.float32), axis=0, keepdims=True)
+        whole = count.astype(jnp.int32)
+        inside = lanes - source * LMAX
+        used = (inside >= 0) & (inside < whole)
+        place_of = jnp.where(used, start + inside, place_of)
+        pos_of = jnp.where(used, inside.astype(jnp.float32), pos_of)
+        len_of = jnp.where(used, count, len_of)
+        start = start + whole
+    take = (
+        lax.broadcasted_iota(jnp.int32, (own, owners * LMAX), 0) == place_of
+    ).astype(jnp.float32)
+    positions = jnp.sum(take * pos_of, axis=1, keepdims=True).astype(jnp.int32)
+    lengths = jnp.sum(take * len_of, axis=1, keepdims=True).astype(jnp.int32)
+    return take.astype(jnp.bfloat16), positions, lengths
 
 
 def dispatch_kernel(
@@ -107,20 +150,7 @@
         pl.semaphore_signal(
             barrier, inc=1, device_id=(flipped(me, j), group), device_id_type=MESH
         )
-    slot = jnp.where(destination[...] < owners, destination[...] * LMAX + position[...], -1)
-    hidden_slot = (order[...] < timestep[...]).astype(jnp.float32)
-
-    def block_for(owner):
-        rows = lax.broadcasted_iota(jnp.int32, (LMAX, slot.shape[1]), 0) + owner * LMAX
-        pick = (rows == slot).astype(jnp.float32)
-        live = jnp.sum(pick, axis=1, keepdims=True)
-        masked = jnp.sum(pick * hidden_slot, axis=1, keepdims=True)
-        block = jnp.dot(
-            pick.astype(jnp.bfloat16), embedded[...], preferred_element_type=jnp.float32
-        )
-        block = jnp.where(masked > 0.5, token[...][None, :].astype(jnp.float32), block)
-        return jnp.where(live > 0.5, block, FILL).astype(jnp.bfloat16)
-
+    block_for = block_builder(owners, destination, position, order, timestep, token, embedded)
     copies = []
     for j in range(owners - 1, 0, -1):
         other = flipped(me, j)
@@ -140,29 +170,11 @@
     got[me] = block_for(me)
     for copy in copies:
         copy.wait_recv()
-    lanes = lax.broadcasted_iota(jnp.int32, (1, owners * LMAX), 1)
-    place_of = jnp.full((1, owners * LMAX), -1, jnp.int32)
-    pos_of = jnp.zeros((1, owners * LMAX), jnp.float32)
-    len_of = jnp.zeros((1, owners * LMAX), jnp.float32)
-    start = jnp.zeros((1, 1), jnp.int32)
-    for source in range(owners):
-        marks = got[source, :, 0:128].astype(jnp.float32)[:, 0:1]
-        count = jnp.sum((marks < FILL / 2).astype(jnp.float32), axis=0, keepdims=True)
-        whole = count.astype(jnp.int32)
-        inside = lanes - source * LMAX
-        used = (inside >= 0) & (inside < whole)
-        place_of = jnp.where(used, start + inside, place_of)
-        pos_of = jnp.where(used, inside.astype(jnp.float32), pos_of)
-        len_of = jnp.where(used, count, len_of)
-        start = start + whole
-    own = bucket.shape[0]
-    take = (
-        lax.broadcasted_iota(jnp.int32, (own, owners * LMAX), 0) == place_of
-    ).astype(jnp.float32)
-    bucket_pos[...] = jnp.sum(take * pos_of, axis=1, keepdims=True).astype(jnp.int32)
-    bucket_len[...] = jnp.sum(take * len_of, axis=1, keepdims=True).astype(jnp.int32)
+    take, positions, lengths = ordering(owners, bucket.shape[0], got)
+    bucket_pos[...] = positions
+    bucket_len[...] = lengths
     bucket[...] = jnp.dot(
-        take.astype(jnp.bfloat16),
+        take,
         got[...].reshape(owners * LMAX, bucket.shape[1]),
         preferred_element_type=jnp.float32,
     ).astype(jnp.bfloat16)
@@ -171,6 +183,9 @@
 
 
 def looped(rows, step, body):
+    while rows % step:
+        step //= 2
+
     def run(i, carry):
         body(pl.ds(pl.multiple_of(i * step, step), step))
         return carry
@@ -392,15 +407,13 @@
 
         lax.fori_loop(0, count, body, 0)
 
-    def advance(part, t):
+    def advance(part, t, picked=(2, 1, 0)):
         half = total >> (t + 2)
-        for c in range(chunks):
+        for c in picked:
             copies[part][c][t].wait_recv()
             nxt = bit_of(*orders[c][t + 1])
             add(part, c, t, (1 - nxt) * half, half)
             copies[part][c][t + 1].start()
-        for c in range(chunks):
-            nxt = bit_of(*orders[c][t + 1])
             add(part, c, t, nxt * half, half)
 
     def finish(part):
@@ -426,7 +439,7 @@
         normal, _ = normalize(owner_input[at, :].astype(jnp.float32))
         first[at, :] = gelu_parts(normal * gain_in[...][None, :])[0].astype(jnp.bfloat16)
 
-    looped(own_rows, 32, first_rows)
+    looped(own_rows, 128, first_rows)
     loads[1].wait()
     hidden[...] = jnp.dot(first[...], weight_in[...], preferred_element_type=jnp.float32)
 
@@ -438,7 +451,7 @@
         mid_gain[at, :] = slope * gain_mid[...][None, :]
         mid_scale[at, :] = scale
 
-    looped(own_rows, 32, mid_rows)
+    looped(own_rows, 128, mid_rows)
     fill_taps(mid, 1)
     pl.semaphore_wait(barrier, steps + 1)
     left_copies[1].start()
@@ -459,7 +472,7 @@
         cot = wide_a[at, :] * slope * gain_out[...][None, :]
         conv_cot[at, :] = pull_back(cot, normal, scale).astype(jnp.bfloat16)
 
-    looped(own_rows, 32, out_rows)
+    looped(own_rows, 128, out_rows)
     turn(right_conv, conv_cot)
     right_copies[0].start()
     turn(right_out, out_act)
@@ -496,7 +509,7 @@
         cot = wide_b[at, :] * mid_gain[at, :]
         hidden_cot[at, :] = pull_back(cot, hidden[at, :], mid_scale[at, :]).astype(jnp.bfloat16)
 
-    looped(own_rows, 32, hidden_rows)
+    looped(own_rows, 128, hidden_rows)
     turn(right_in, hidden_cot)
     right_copies[2].start()
     halves = weight_in.shape[0] // 2
@@ -520,21 +533,439 @@
             jnp.bfloat16
         )
 
-    def late_rows(at):
-        input_rows(pl.ds(pl.multiple_of(at.start + own_rows // 2, 32), 32))
-
-    advance(0, 0)
-    looped(own_rows // 2, 32, input_rows)
-    advance(0, 1)
-    advance(1, 0)
-    looped(own_rows // 2, 32, late_rows)
+    quarter = own_rows // 4
+
+    def input_quarter(n):
+        def some(at):
+            input_rows(pl.ds(pl.multiple_of(at.start + n * quarter, 32), 32))
+
+        looped(quarter, 32, some)
+
+    advance(0, 0, (2,))
+    advance(0, 0, (1,))
+    input_quarter(0)
+    advance(0, 0, (0,))
+    advance(1, 0, (2,))
+    input_quarter(1)
+    advance(1, 0, (1,))
+    advance(0, 1, (2,))
+    input_quarter(2)
+    advance(1, 0, (0,))
+    advance(0, 1, (0,))
+    input_quarter(3)
+    advance(0, 1, (1,))
     for t in range(2, steps):
+        advance(1, t - 1, (2,))
         if t < steps - 1:
-            advance(0, t)
-        advance(1, t - 1)
+            advance(0, t, (2,))
+        advance(1, t - 1, (0,))
+        if t < steps - 1:
+            advance(0, t, (0,))
+        advance(1, t - 1, (1,))
+        if t < steps - 1:
+            advance(0, t, (1,))
     early_sum[...] = finish(0)
     late_sum[...] = finish(1)
     for copy in left_copies + right_copies:
+        copy.wait_send()
+    for part in range(2):
+        for c in range(chunks):
+            for t in range(steps):
+                copies[part][c][t].wait_send()
+
+
+def fused_kernel(
+    owners,
+    groups,
+    destination,
+    place,
+    order,
+    timestep,
+    token,
+    embedded,
+    upstream,
+    gain_in,
+    gain_mid,
+    gain_out,
+    weight_in_hbm,
+    weight_conv_hbm,
+    weight_out_hbm,
+    grad_input,
+    early_sum,
+    late_sum,
+    *scratch,
+):
+    chunks = 3
+    terms = (scratch[0:3], scratch[3:6])
+    got = (scratch[6:9], scratch[9:12])
+    left_conv, left_out, left_last, left_in = scratch[12:16]
+    right_conv, right_out, right_in = scratch[16:19]
+    weight_in, weight_conv, weight_out = scratch[19:22]
+    first, mid, out_act, conv_cot, hidden_cot, taps = scratch[22:28]
+    hidden, mid_gain, mid_scale, wide_a, wide_b = scratch[28:33]
+    right_conv_peer, right_out_peer, right_in_peer = scratch[33:36]
+    send_sem, recv_sem, load_sem, factor_send, factor_recv = scratch[36:41]
+    sent, arrived, arrived_act, owner_input, taken, position, length = scratch[41:48]
+    block_send, block_recv = scratch[48:50]
+
+    orders = bit_orders(owners, groups)
+    steps = len(orders[0])
+    total = 1 << steps
+    me = {"dp": lax.axis_index("dp"), "shard": lax.axis_index("shard")}
+    own_rows = upstream.shape[0]
+    narrow, wide = mid.shape[1] // owners, first.shape[1] // owners
+    rows = right_conv.shape[2]
+    layouts = part_layouts(narrow, wide)
+
+    def bit_of(axis, bit):
+        return lax.rem(me[axis] // (1 << bit), 2)
+
+    def partner(axis, bit):
+        other = me[axis] + (1 - 2 * bit_of(axis, bit)) * (1 << bit)
+        return (other, me["shard"]) if axis == "dp" else (me["dp"], other)
+
+    loads = [
+        pltpu.make_async_copy(source, target, load_sem.at[i])
+        for i, (source, target) in enumerate(
+            (
+                (weight_out_hbm, weight_out),
+                (weight_in_hbm, weight_in),
+                (weight_conv_hbm, weight_conv),
+            )
+        )
+    ]
+    for load in loads:
+        load.start()
+    barrier = pltpu.get_barrier_semaphore()
+    near = [item for item in [("shard", 0)] + orders[0] if item[0] == "shard"]
+    for axis, bit in near:
+        pl.semaphore_signal(barrier, inc=1, device_id=partner(axis, bit), device_id_type=MESH)
+    for j in range(1, owners):
+        other = (flipped(me["dp"], j), me["shard"])
+        pl.semaphore_signal(barrier, inc=1, device_id=other, device_id_type=MESH)
+    blocks = block_builder(owners, destination, place, order, timestep, token, embedded)
+    block_copies = {}
+    half, quarter = owners // 2, owners // 4
+    near_blocks = [j for j in range(2, half)] + [1]
+    first_far = list(range(half, half + quarter))
+    last_far = list(range(half + quarter, owners))
+    send_order = list(dict.fromkeys(first_far + near_blocks + last_far))
+    for j in send_order:
+        other = flipped(me["dp"], j)
+        sent[j] = blocks(other)
+        if j == send_order[0]:
+            pl.semaphore_wait(barrier, owners - 1 + len(near))
+        block_copies[j] = pltpu.make_async_remote_copy(
+            src_ref=sent.at[j],
+            dst_ref=arrived.at[me["dp"]],
+            send_sem=block_send.at[j],
+            recv_sem=block_recv.at[j],
+            device_id=(other, me["shard"]),
+            device_id_type=MESH,
+        )
+        block_copies[j].start()
+    arrived[me["dp"]] = blocks(me["dp"])
+    core = bit_of("shard", 0)
+
+    def to_other_core(number, source, target):
+        return pltpu.make_async_remote_copy(
+            src_ref=source,
+            dst_ref=target,
+            send_sem=factor_send.at[number],
+            recv_sem=factor_recv.at[number],
+            device_id=partner("shard", 0),
+            device_id_type=MESH,
+        )
+
+    lefts = (left_conv, left_out, left_last, left_in)
+    left_copies = [to_other_core(n, ref.at[0], ref.at[1]) for n, ref in enumerate(lefts)]
+    rights = ((right_conv, right_conv_peer), (right_out, right_out_peer), (right_in, right_in_peer))
+    right_copies = [
+        to_other_core(4 + n, ref.at[1 - core], peer) for n, (ref, peer) in enumerate(rights)
+    ]
+
+    def turn(right, values):
+        turned = values[...].T
+        for g in range(groups):
+            right[g % 2, g // 2] = turned[g * rows : (g + 1) * rows]
+
+    tap_offsets = [(k - KERNEL_TAPS // 2) * DILATION_STEP for k in range(KERNEL_TAPS)]
+
+    def fill_taps(source, sign):
+        for k, base_offset in enumerate(tap_offsets):
+            offset = sign * base_offset
+            moved = position[...] + offset
+            valid = (moved >= 0) & (moved < length[...])
+            shifted = raw_shift(source[...], offset)
+            taps[k] = jnp.where(valid, shifted.astype(jnp.float32), 0.0).astype(jnp.bfloat16)
+
+    def place(left, pieces, offset):
+        for owner in range(owners):
+            values = pieces(owner)
+            left[0, owner] = placed(values, offset)[1].astype(jnp.bfloat16)
+
+    def wide_piece(source):
+        return lambda owner: source[:, owner * wide : (owner + 1) * wide].astype(jnp.float32)
+
+    def multiply(part, low_bit, sides):
+        outs = terms[part]
+        width = outs[0].shape[2]
+
+        def body(pair, carry):
+            owner = pair * 2 + low_bit
+            tiles = [None] * (width // 128)
+            for left, (right, peer), offset in sides:
+                low = offset // 128
+                picked = jnp.concatenate(
+                    [
+                        right[core].reshape(groups // 2 * rows, own_rows),
+                        peer[...].reshape(groups // 2 * rows, own_rows),
+                    ],
+                    axis=1,
+                )
+                both = jnp.concatenate([left[0, owner], left[1, owner]], axis=0)
+                term = jnp.dot(picked, both, preferred_element_type=jnp.float32)
+                for j in range(left.shape[3] // 128):
+                    piece = term[:, j * 128 : (j + 1) * 128]
+                    held = tiles[low + j]
+                    tiles[low + j] = piece if held is None else held + piece
+            for j, tile in enumerate(tiles):
+                tile = tile.astype(jnp.bfloat16)
+                for i in range(groups // 2):
+                    at = i * rows
+                    for order, out in zip(orders, outs):
+                        index = 0
+                        for axis, bit in order:
+                            if axis == "dp":
+                                index = index * 2 + lax.rem(owner // (1 << bit), 2)
+                            else:
+                                index = index * 2 + ((i >> (bit - 1)) & 1)
+                        count = out.shape[1]
+                        out[index, :, j * 128 : (j + 1) * 128] = tile[at : at + count]
+                        at += count
+            return carry
+
+        lax.fori_loop(0, owners // 2, body, 0)
+
+    base, at = [], 0
+    for t in range(steps):
+        base.append(at)
+        at += total >> (t + 1)
+
+    def copy_of(part, c, t):
+        half = total >> (t + 1)
+        away = 1 - bit_of(*orders[c][t])
+        source = terms[part][c] if t == 0 else got[part][c]
+        start = away * half if t == 0 else base[t - 1] + away * half
+        return pltpu.make_async_remote_copy(
+            src_ref=source.at[pl.ds(start, half)],
+            dst_ref=got[part][c].at[pl.ds(base[t], half)],
+            send_sem=send_sem.at[part, c, t],
+            recv_sem=recv_sem.at[part, c, t],
+            device_id=partner(*orders[c][t]),
+            device_id_type=MESH,
+        )
+
+    copies = [
+        [[copy_of(part, c, t) for t in range(steps)] for c in range(chunks)] for part in range(2)
+    ]
+
+    def summed(part, c, t, at):
+        half = total >> (t + 1)
+        kept = bit_of(*orders[c][t]) * half
+        source = terms[part][c] if t == 0 else got[part][c]
+        offset = kept if t == 0 else base[t - 1] + kept
+        here = got[part][c]
+        return source[offset + at].astype(jnp.float32) + here[base[t] + at].astype(jnp.float32)
+
+    def add(part, c, t, first_block, count):
+        def body(i, carry):
+            at = first_block + i
+            got[part][c][base[t] + at] = summed(part, c, t, at).astype(jnp.bfloat16)
+            return carry
+
+        lax.fori_loop(0, count, body, 0)
+
+    def advance(part, t, picked=(2, 1, 0)):
+        half = total >> (t + 2)
+        for c in picked:
+            copies[part][c][t].wait_recv()
+            nxt = bit_of(*orders[c][t + 1])
+            add(part, c, t, (1 - nxt) * half, half)
+            copies[part][c][t + 1].start()
+            add(part, c, t, nxt * half, half)
+
+    def finish(part):
+        finished = []
+        for c in range(chunks):
+            copies[part][c][steps - 1].wait_recv()
+            finished.append(summed(part, c, steps - 1, 0))
+        return jnp.concatenate(finished, axis=0)
+
+    def tap_piece(ks):
+        def piece(owner):
+            here = slice(owner * narrow, (owner + 1) * narrow)
+            parts = [taps[k, :, here].astype(jnp.float32) for k in ks]
+            return parts[0] if len(parts) == 1 else jnp.concatenate(parts, axis=1)
+
+        return piece
+
+    place(left_out, wide_piece(upstream), layouts[0][1][0])
+    loads[0].wait()
+    wide_a[...] = jnp.dot(upstream[...], weight_out[...], preferred_element_type=jnp.float32)
+
+    def activate(source):
+        def block_rows(at):
+            normal, _ = normalize(arrived[source, at, :].astype(jnp.float32))
+            act = gelu_parts(normal * gain_in[...][None, :])[0]
+            arrived_act[source, at, :] = act.astype(jnp.bfloat16)
+
+        looped(LMAX, 16, block_rows)
+
+    activate(me["dp"])
+    for j in dict.fromkeys(near_blocks + first_far + last_far):
+        block_copies[j].wait_recv()
+        activate(flipped(me["dp"], j))
+    take, positions, lengths = ordering(owners, own_rows, arrived)
+    position[...] = positions
+    length[...] = lengths
+    taken[...] = take
+    first[...] = jnp.dot(
+        take,
+        arrived_act[...].reshape(owners * LMAX, first.shape[1]),
+        preferred_element_type=jnp.float32,
+    ).astype(jnp.bfloat16)
+    loads[1].wait()
+    hidden[...] = jnp.dot(first[...], weight_in[...], preferred_element_type=jnp.float32)
+
+    def mid_rows(at):
+        normal, scale = normalize(hidden[at, :])
+        act, slope = gelu_parts(normal * gain_mid[...][None, :])
+        mid[at, :] = act.astype(jnp.bfloat16)
+        hidden[at, :] = normal
+        mid_gain[at, :] = slope * gain_mid[...][None, :]
+        mid_scale[at, :] = scale
+
+    looped(own_rows, 128, mid_rows)
+    fill_taps(mid, 1)
+    left_copies[1].start()
+    place(left_conv, tap_piece(range(KERNEL_TAPS - 1)), layouts[0][0][0])
+    left_copies[0].start()
+    place(left_last, tap_piece((KERNEL_TAPS - 1,)), layouts[1][0][0])
+    left_copies[2].start()
+    loads[2].wait()
+    conv = jnp.dot(taps[0], weight_conv[0], preferred_element_type=jnp.float32)
+    for k in range(1, KERNEL_TAPS):
+        conv = conv + jnp.dot(taps[k], weight_conv[k], preferred_element_type=jnp.float32)
+    wide_b[...] = conv
+
+    def out_rows(at):
+        normal, scale = normalize(wide_b[at, :])
+        act, slope = gelu_parts(normal * gain_out[...][None, :])
+        out_act[at, :] = act.astype(jnp.bfloat16)
+        cot = wide_a[at, :] * slope * gain_out[...][None, :]
+        conv_cot[at, :] = pull_back(cot, normal, scale).astype(jnp.bfloat16)
+
+    looped(own_rows, 128, out_rows)
+    turn(right_conv, conv_cot)
+    right_copies[0].start()
+    turn(right_out, out_act)
+    right_copies[1].start()
+    fill_taps(conv_cot, -1)
+    place(left_in, wide_piece(first), layouts[1][1][0])
+    left_copies[3].start()
+    side_bit = bit_of(*orders[1][0])
+    sides = (
+        (
+            (left_conv, rights[0], layouts[0][0][0]),
+            (left_out, rights[1], layouts[0][1][0]),
+        ),
+        (
+            (left_last, rights[0], layouts[1][0][0]),
+            (left_in, rights[2], layouts[1][1][0]),
+        ),
+    )
+    left_copies[1].wait_recv()
+    left_copies[0].wait_recv()
+    right_copies[0].wait_recv()
+    right_copies[1].wait_recv()
+    multiply(0, 1 - side_bit, sides[0])
+    copies[0][1][0].start()
+    multiply(0, side_bit, sides[0])
+    copies[0][0][0].start()
+    copies[0][2][0].start()
+    mid_cot = contract_cols(taps[0], weight_conv[0])
+    for k in range(1, KERNEL_TAPS):
+        mid_cot = mid_cot + contract_cols(taps[k], weight_conv[k])
+    wide_b[...] = mid_cot
+
+    def hidden_rows(at):
+        cot = wide_b[at, :] * mid_gain[at, :]
+        hidden_cot[at, :] = pull_back(cot, hidden[at, :], mid_scale[at, :]).astype(jnp.bfloat16)
+
+    looped(own_rows, 128, hidden_rows)
+    turn(right_in, hidden_cot)
+    right_copies[2].start()
+    halves = weight_in.shape[0] // 2
+    wide_a[...] = contract_cols(hidden_cot[...], weight_in[:halves])
+    left_copies[2].wait_recv()
+    left_copies[3].wait_recv()
+    right_copies[2].wait_recv()
+    multiply(1, 1 - side_bit, sides[1])
+    copies[1][1][0].start()
+    multiply(1, side_bit, sides[1])
+    copies[1][0][0].start()
+    copies[1][2][0].start()
+    wide_b[...] = contract_cols(hidden_cot[...], weight_in[halves:])
+
+    def input_rows(start):
+        piece = jnp.concatenate([wide_a[start, :], wide_b[start, :]], axis=1)
+        normal, scale = normalize(owner_input[start, :].astype(jnp.float32))
+        slope = gelu_parts(normal * gain_in[...][None, :])[1]
+        grad = pull_back(piece * slope * gain_in[...][None, :], normal, scale)
+        grad_input[start, :] = (upstream[start, :].astype(jnp.float32) + grad).astype(
+            jnp.bfloat16
+        )
+
+    piece_rows = own_rows // 4
+
+    def input_quarter(n):
+        def some(at):
+            input_rows(pl.ds(pl.multiple_of(at.start + n * piece_rows, 32), 32))
+
+        looped(piece_rows, 32, some)
+
+    owner_input[...] = jnp.dot(
+        taken[...],
+        arrived[...].reshape(owners * LMAX, first.shape[1]),
+        preferred_element_type=jnp.float32,
+    ).astype(jnp.bfloat16)
+    advance(0, 0, (2,))
+    advance(0, 0, (1,))
+    input_quarter(0)
+    advance(0, 0, (0,))
+    advance(1, 0, (2,))
+    input_quarter(1)
+    advance(1, 0, (1,))
+    advance(0, 1, (2,))
+    input_quarter(2)
+    advance(1, 0, (0,))
+    advance(0, 1, (0,))
+    input_quarter(3)
+    advance(0, 1, (1,))
+    for t in range(2, steps):
+        advance(1, t - 1, (2,))
+        if t < steps - 1:
+            advance(0, t, (2,))
+        advance(1, t - 1, (0,))
+        if t < steps - 1:
+            advance(0, t, (0,))
+        advance(1, t - 1, (1,))
+        if t < steps - 1:
+            advance(0, t, (1,))
+    early_sum[...] = finish(0)
+    late_sum[...] = finish(1)
+    for copy in list(block_copies.values()) + left_copies + right_copies:
         copy.wait_send()
     for part in range(2):
         for c in range(chunks):
@@ -578,46 +1009,18 @@
     own_rows = upstream.shape[0]
     inner = weight_in.shape[1]
     vmem = pl.BlockSpec(memory_space=pltpu.VMEM)
-    bucket, bucket_pos, bucket_len = pl.pallas_call(
-        functools.partial(dispatch_kernel, owners),
-        out_shape=[
-            jax.ShapeDtypeStruct((own_rows, channels), jnp.bfloat16),
-            jax.ShapeDtypeStruct((own_rows, 1), jnp.int32),
-            jax.ShapeDtypeStruct((own_rows, 1), jnp.int32),
-        ],
-        in_specs=[vmem] * 6,
-        out_specs=[vmem] * 3,
-        scratch_shapes=[
-            pltpu.VMEM((owners, LMAX, channels), jnp.bfloat16),
-            pltpu.VMEM((owners, LMAX, channels), jnp.bfloat16),
-            pltpu.SemaphoreType.DMA((owners,)),
-            pltpu.SemaphoreType.DMA((owners,)),
-        ],
-        compiler_params=pltpu.CompilerParams(
-            collective_id=1, has_side_effects=True, vmem_limit_bytes=VMEM_LIMIT
-        ),
-        name="dispatch",
-    )(
-        destination[None, :],
-        position[None, :],
-        unmask_order[None, :],
-        timestep[None, :],
-        mask_token_embedding,
-        embedded,
-    )
     narrow, wide, rows = inner // owners, channels // owners, inner // groups
     layouts = part_layouts(narrow, wide)
     total = owners * groups // 2
     steps = total.bit_length() - 1
     counts = chunk_rows(rows)
     hbm = pl.BlockSpec(memory_space=pl.ANY)
-    partial_results = pl.pallas_call(
-        functools.partial(layer_kernel, owners, groups),
-        out_shape=[jax.ShapeDtypeStruct((own_rows, channels), jnp.bfloat16)]
-        + [jax.ShapeDtypeStruct((rows, width_of(layout)), jnp.float32) for layout in layouts],
-        in_specs=[vmem] * 7 + [hbm] * 3,
-        out_specs=[vmem] * 3,
-        scratch_shapes=[
+    weights = (weight_in, jnp.transpose(weight_conv, (1, 0, 2)), weight_out)
+    results = [jax.ShapeDtypeStruct((own_rows, channels), jnp.bfloat16)] + [
+        jax.ShapeDtypeStruct((rows, width_of(layout)), jnp.float32) for layout in layouts
+    ]
+    scratch = (
+        [
             pltpu.VMEM((total, n, width_of(layout)), jnp.bfloat16)
             for layout in layouts
             for n in counts
@@ -655,23 +1058,83 @@
             pltpu.SemaphoreType.DMA((3,)),
             pltpu.SemaphoreType.DMA((7,)),
             pltpu.SemaphoreType.DMA((7,)),
-        ],
-        compiler_params=pltpu.CompilerParams(
-            collective_id=0, has_side_effects=True, vmem_limit_bytes=VMEM_LIMIT
-        ),
-        name="layer",
-    )(
-        bucket_pos,
-        bucket_len,
-        bucket,
-        upstream,
-        gain_in,
-        gain_mid,
-        gain_out,
-        weight_in,
-        jnp.transpose(weight_conv, (1, 0, 2)),
-        weight_out,
+        ]
     )
+    block_bytes = 2 * owners * LMAX * channels
+    if 3 * block_bytes <= BLOCK_LIMIT:
+        partial_results = pl.pallas_call(
+            functools.partial(fused_kernel, owners, groups),
+            out_shape=results,
+            in_specs=[vmem] * 10 + [hbm] * 3,
+            out_specs=[vmem] * 3,
+            scratch_shapes=scratch
+            + [pltpu.VMEM((owners, LMAX, channels), jnp.bfloat16)] * 3
+            + [
+                pltpu.VMEM((own_rows, channels), jnp.bfloat16),
+                pltpu.VMEM((own_rows, owners * LMAX), jnp.bfloat16),
+                pltpu.VMEM((own_rows, 1), jnp.int32),
+                pltpu.VMEM((own_rows, 1), jnp.int32),
+                pltpu.SemaphoreType.DMA((owners,)),
+                pltpu.SemaphoreType.DMA((owners,)),
+            ],
+            compiler_params=pltpu.CompilerParams(
+                collective_id=0, has_side_effects=True, vmem_limit_bytes=VMEM_LIMIT
+            ),
+            name="layer",
+        )(
+            destination[None, :],
+            position[None, :],
+            unmask_order[None, :],
+            timestep[None, :],
+            mask_token_embedding,
+            embedded,
+            upstream,
+            gain_in,
+            gain_mid,
+            gain_out,
+            *weights,
+        )
+    else:
+        bucket, bucket_pos, bucket_len = pl.pallas_call(
+            functools.partial(dispatch_kernel, owners),
+            out_shape=[
+                jax.ShapeDtypeStruct((own_rows, channels), jnp.bfloat16),
+                jax.ShapeDtypeStruct((own_rows, 1), jnp.int32),
+                jax.ShapeDtypeStruct((own_rows, 1), jnp.int32),
+            ],
+            in_specs=[vmem] * 6,
+            out_specs=[vmem] * 3,
+            scratch_shapes=[
+                pltpu.VMEM((owners, LMAX, channels), jnp.bfloat16),
+                pltpu.VMEM((owners, LMAX, channels), jnp.bfloat16),
+                pltpu.SemaphoreType.DMA((owners,)),
+                pltpu.SemaphoreType.DMA((owners,)),
+            ],
+            compiler_params=pltpu.CompilerParams(
+                collective_id=1, has_side_effects=True, vmem_limit_bytes=VMEM_LIMIT
+            ),
+            name="dispatch",
+        )(
+            destination[None, :],
+            position[None, :],
+            unmask_order[None, :],
+            timestep[None, :],
+            mask_token_embedding,
+            embedded,
+        )
+        partial_results = pl.pallas_call(
+            functools.partial(layer_kernel, owners, groups),
+            out_shape=results,
+            in_specs=[vmem] * 7 + [hbm] * 3,
+            out_specs=[vmem] * 3,
+            scratch_shapes=scratch,
+            compiler_params=pltpu.CompilerParams(
+                collective_id=0, has_side_effects=True, vmem_limit_bytes=VMEM_LIMIT
+            ),
+            name="layer",
+        )(
+            bucket_pos, bucket_len, bucket, upstream, gain_in, gain_mid, gain_out, *weights
+        )
     grad_input, grad_in, grad_conv, grad_out = pl.pallas_call(
         functools.partial(result_kernel, layouts),
         out_shape=[

time: 119 us -> 106 us (0.89)
  Pallas kernels: 119 us -> 105 us
    pallas_call x2 -> x1, Pallas kernels: 116 us -> 103 us  [local(): pl.pallas_call(functools.partial(fused_kernel, owners, groups), out_shape...]
where the time goes in v3:
time: 106 us
  Pallas kernels  105 us (99%)
    pallas_call x1, Pallas kernels, local(): pl.pallas_call(functools.partial(fused_kernel, owners, groups), out_shape...  103 us
    pallas_call x1, Pallas kernels, local(): pl.pallas_call(functools.partial(result_kernel, layouts), out_shape=[jax....  2.7 us

profile of v3, /device:TPU:0, one launch (start us, length us, event | category | flops | bytes accessed | tf_op | source)
XLA Modules:
  0.0 106.0 jit_solution(13556685039576503831)
XLA Ops:
  0.6 102.7 %layer.1 = (bf16[384,1280]{1,0:T(8,128)(2,1)}, f32[160,512]{1,0:T(8,128)}, f32[160,256]{1,0:T(8,128)}) custom-call(s32[1,960]{1,0:T(1,128)} %bitcast.7, s32[1,960]{1,0:T(1,128)} %bitcast.8, s32[1,960]{1,0:T(1,128)} %bitcast.9, s32[1,960]{1,0:T(1,128)} %bitcast.10, bf16[1280]{0:T(1024)(128)(2,1)} %token_.1, bf16[960,1280]{1,0:T(8,128)(2,1)} %embedded.1, ...), custom_call_target="tpu_custom_call" | custom-call | tf_op jit(solution)/shard_map/layer/pallas_call | solution.py:1065
  103.3 2.7 %results.1 = (bf16[384,1280]{1,0:T(8,128)(2,1)}, f32[160,160]{1,0:T(8,128)}, f32[5,80,160]{2,1,0:T(8,128)}, f32[160,160]{1,0:T(8,128)}) custom-call(bf16[384,1280]{1,0:T(8,128)(2,1)} %get-tuple-element.11.grad_rows, f32[160,512]{1,0:T(8,128)} %get-tuple-element.12.early_sum, f32[160,256]{1,0:T(8,128)} %get-tuple-element.13.late_sum), custom_call_target="tpu_custom_call" | custom-call | tf_op jit(solution)/shard_map/results/pallas_call | solution.py:1138
